TPU v7x, 32 devices: a whole 2x2x4 slice. The times are simulated.
32 devices in a mesh: dp: 8 (over z, x), mp: 4 (over y, core).
Axes of the slice: x: 2, y: 2, z: 4, core: 2. Of those that a mesh axis runs over, the one named last changes fastest.
Arguments:
- tokens: bfloat16 [13312, 768], P(('dp', 'mp')), may hold values from -6 to 6
- lengths: int32 [8, 3], P('dp'), may hold values from 100 to 781, as said below
- cotangent: bfloat16 [13312, 768], P(('dp', 'mp')), may hold values from -6 to 6
- qkv_weight: float32 [3, 768, 768], P(None, 'dp', 'mp'), may hold values from -0.21875 to 0.21875
- out_weight: float32 [768, 768], P('mp', 'dp'), may hold values from -0.875 to 0.875
- up_weight: float32 [768, 3072], P('dp', 'mp'), may hold values from -0.21875 to 0.21875
- down_weight: float32 [3072, 768], P('mp', 'dp'), may hold values from -0.109375 to 0.109375
- head_bias: float32 [2, 768], P(None, 'mp'), may hold values from -4 to 4
- up_bias: float32 [3072], P('mp'), may hold values from -6 to 6
- norm_vectors: float32 [6, 768], replicated, may hold values from -1.2 to 1.6
- qkv_moment: float32 [3, 768, 768], P(None, 'dp', 'mp'), may hold values from -160 to 160
- out_moment: float32 [768, 768], P('mp', 'dp'), may hold values from -160 to 160
- up_moment: float32 [768, 3072], P('dp', 'mp'), may hold values from -160 to 160
- down_moment: float32 [3072, 768], P('mp', 'dp'), may hold values from -160 to 160
- head_bias_moment: float32 [2, 768], P(None, 'mp'), may hold values from -160 to 160
- up_bias_moment: float32 [3072], P('mp'), may hold values from -160 to 160
- norm_moment: float32 [6, 768], replicated, may hold values from -160 to 160
- qkv_average: float32 [3, 768, 768], P(None, 'dp', 'mp'), may hold values from -0.21875 to 0.21875
- out_average: float32 [768, 768], P('mp', 'dp'), may hold values from -0.875 to 0.875
- up_average: float32 [768, 3072], P('dp', 'mp'), may hold values from -0.21875 to 0.21875
- down_average: float32 [3072, 768], P('mp', 'dp'), may hold values from -0.109375 to 0.109375
- head_bias_average: float32 [2, 768], P(None, 'mp'), may hold values from -4 to 4
- up_bias_average: float32 [3072], P('mp'), may hold values from -6 to 6
- norm_average: float32 [6, 768], replicated, may hold values from -1.2 to 1.6
Outputs:
- layer_out: bfloat16 [13312, 768], P(('dp', 'mp'))
- tokens_grad: float32 [13312, 768], P(('dp', 'mp'))
- qkv_grad: float32 [3, 768, 768], P(None, 'dp', 'mp')
- out_grad: float32 [768, 768], P('mp', 'dp')
- up_grad: float32 [768, 3072], P('dp', 'mp')
- down_grad: float32 [3072, 768], P('mp', 'dp')
- head_bias_grad: float32 [2, 768], P(None, 'mp')
- up_bias_grad: float32 [3072], P('mp')
- norm_grad: float32 [6, 768], replicated
- qkv_next: float32 [3, 768, 768], P(None, 'dp', 'mp')
- out_next: float32 [768, 768], P('mp', 'dp')
- up_next: float32 [768, 3072], P('dp', 'mp')
- down_next: float32 [3072, 768], P('mp', 'dp')
- head_bias_next: float32 [2, 768], P(None, 'mp')
- up_bias_next: float32 [3072], P('mp')
- norm_next: float32 [6, 768], replicated
- qkv_moment_next: float32 [3, 768, 768], P(None, 'dp', 'mp')
- out_moment_next: float32 [768, 768], P('mp', 'dp')
- up_moment_next: float32 [768, 3072], P('dp', 'mp')
- down_moment_next: float32 [3072, 768], P('mp', 'dp')
- head_bias_moment_next: float32 [2, 768], P(None, 'mp')
- up_bias_moment_next: float32 [3072], P('mp')
- norm_moment_next: float32 [6, 768], replicated
- qkv_average_next: float32 [3, 768, 768], P(None, 'dp', 'mp')
- out_average_next: float32 [768, 768], P('mp', 'dp')
- up_average_next: float32 [768, 3072], P('dp', 'mp')
- down_average_next: float32 [3072, 768], P('mp', 'dp')
- head_bias_average_next: float32 [2, 768], P(None, 'mp')
- up_bias_average_next: float32 [3072], P('mp')
- norm_average_next: float32 [6, 768], replicated
Inputs may be any that keep to these rules, and one draw needn't show every extreme that they name: Column b holds the lengths of bucket b: from 100 to 200, 200 to 400, 390 to 781; in every draw some utterance of each bucket has the bucket's most.
All inputs are finite; a program needn't handle non-finite values.
Results may differ from a plain program's by a relative error of at most 0.018.
Values may be sent and summed in bfloat16 or wider, within the bound.
A program may use at most 128 MiB of HBM per device.

v0:
```python
from functools import partial
import math

import jax
import jax.numpy as jnp
from jax import lax
from jax.sharding import PartitionSpec as P

HEAD_DIM = 64
UTT = 1
LEN1 = 256
LEN2 = 512
LEN3 = 896


EPS = 1e-05
MOMENTUM = 0.5
DECAY = 0.5
RATE_SCALES = (0.02, 0.16, 0.02, 0.02, 0.02, 0.32, 0.16)
NEG_FILL = -1000000000.0


def layer_norm(values, gain_vec, shift_vec):
    center = values - jnp.mean(values, axis=-1, keepdims=True)
    spread = jnp.mean(center * center, axis=-1, keepdims=True)
    return center * lax.rsqrt(spread + EPS) * gain_vec + shift_vec


def bucket_list():
    listing = []
    offset = 0
    for bucket, extent in enumerate((LEN1, LEN2, LEN3)):
        listing.append((bucket, offset, extent))
        offset += UTT * extent
    return listing


def row_valid(lengths):
    pieces = []
    for bucket, offset, extent in bucket_list():
        inside = jnp.arange(extent)[None, :] < lengths[:, bucket][:, None]
        pieces.append(inside.astype(jnp.float32).reshape(UTT * extent))
    return jnp.concatenate(pieces)


def head_split(block_qkv, extent):
    return block_qkv.reshape(3, UTT, extent, block_qkv.shape[-1] // HEAD_DIM, HEAD_DIM)


def masked_scores(block_qkv, lengths, bucket, extent):
    inside = jnp.arange(extent)[None, :] < lengths[:, bucket][:, None]
    scores = jnp.einsum(
        "uqhd,ukhd->uhqk", block_qkv[0], block_qkv[1], preferred_element_type=jnp.float32
    ) * HEAD_DIM ** (-0.5)
    return jnp.where(inside[:, None, None, :], scores, NEG_FILL)


def attend_forward(qkv_act, lengths):
    outputs, log_sums = ([], [])
    for bucket, offset, extent in bucket_list():
        block_qkv = head_split(qkv_act[:, offset : offset + UTT * extent], extent)
        scores = masked_scores(block_qkv, lengths, bucket, extent)
        row_peak = jnp.max(scores, axis=-1, keepdims=True)
        exp_scores = jnp.exp(scores - row_peak)
        row_total = jnp.sum(exp_scores, axis=-1, keepdims=True)
        prob_low = (exp_scores / row_total).astype(jnp.bfloat16)
        output = jnp.einsum(
            "uhqk,ukhd->uqhd", prob_low, block_qkv[2], preferred_element_type=jnp.float32
        )
        outputs.append(output.reshape(UTT * extent, -1))
        log_sums.append(row_peak + jnp.log(row_total))
    return (jnp.concatenate(outputs, 0), log_sums)


def attend_backward(qkv_act, lengths, log_sums, d_attn):
    score_scale = HEAD_DIM ** (-0.5)
    grad_parts = []
    for (bucket, offset, extent), log_sum in zip(bucket_list(), log_sums):
        block_qkv = head_split(qkv_act[:, offset : offset + UTT * extent], extent)
        d_out = d_attn[offset : offset + UTT * extent].reshape(UTT, extent, -1, HEAD_DIM)
        scores = masked_scores(block_qkv, lengths, bucket, extent)
        prob_full = jnp.exp(scores - log_sum)
        prob_low = prob_full.astype(jnp.bfloat16)
        d_vals = jnp.einsum("uhqk,uqhd->ukhd", prob_low, d_out, preferred_element_type=jnp.float32)
        d_prob = jnp.einsum(
            "uqhd,ukhd->uhqk", d_out, block_qkv[2], preferred_element_type=jnp.float32
        )
        d_scores = prob_full * (d_prob - jnp.sum(prob_full * d_prob, axis=-1, keepdims=True))
        d_low = d_scores.astype(jnp.bfloat16)
        d_query = (
            jnp.einsum("uhqk,ukhd->uqhd", d_low, block_qkv[1], preferred_element_type=jnp.float32)
            * score_scale
        )
        d_keys = (
            jnp.einsum("uhqk,uqhd->ukhd", d_low, block_qkv[0], preferred_element_type=jnp.float32)
            * score_scale
        )
        grad_parts.append(jnp.stack([d_query, d_keys, d_vals]).reshape(3, UTT * extent, -1))
    return jnp.concatenate(grad_parts, 1)


def update_one(rate, weight, grad, moment, average):
    moment_next = MOMENTUM * moment + grad
    weight_next = weight - rate * (grad + MOMENTUM * moment_next)
    return (weight_next, moment_next, DECAY * average + (1.0 - DECAY) * weight_next)


def on_device(
    tokens,
    lengths,
    cotangent,
    qkv_weight,
    out_weight,
    up_weight,
    down_weight,
    head_bias,
    up_bias,
    norm_vectors,
    qkv_moment,
    out_moment,
    up_moment,
    down_moment,
    head_bias_moment,
    up_bias_moment,
    norm_moment,
    qkv_average,
    out_average,
    up_average,
    down_average,
    head_bias_average,
    up_bias_average,
    norm_average,
):
    data_size = lax.axis_size("dp")
    model_size = lax.axis_size("mp")
    model_rank = lax.axis_index("mp")
    rows_local = tokens.shape[0]
    qkv_low, out_low, up_low, down_low = (
        lax.all_gather(qkv_weight.astype(jnp.bfloat16), "dp", axis=1, tiled=True),
        lax.all_gather(out_weight.astype(jnp.bfloat16), "dp", axis=1, tiled=True),
        lax.all_gather(up_weight.astype(jnp.bfloat16), "dp", axis=0, tiled=True),
        lax.all_gather(down_weight.astype(jnp.bfloat16), "dp", axis=1, tiled=True),
    )
    head_width = qkv_low.shape[2]
    unit_width = up_low.shape[1]
    valid_all = row_valid(lengths)
    valid_own = lax.dynamic_slice_in_dim(valid_all, model_rank * rows_local, rows_local)[:, None]
    tokens_wide = tokens.astype(jnp.float32)

    def attention_block(tokens_all):
        bias_rows = jnp.stack([head_bias[0], jnp.zeros_like(head_bias[0]), head_bias[1]])
        qkv_full = (
            jnp.einsum("td,cde->cte", tokens_all, qkv_low, preferred_element_type=jnp.float32)
            + bias_rows[:, None, :]
        )
        qkv_act = qkv_full.astype(jnp.bfloat16)
        attn, log_sums = attend_forward(qkv_act, lengths)
        return (qkv_act, attn.astype(jnp.bfloat16), log_sums)

    def feed_block(first_all):
        pre = jnp.dot(first_all, up_low, preferred_element_type=jnp.float32) + up_bias
        return (pre, jax.nn.gelu(pre, approximate=False).astype(jnp.bfloat16))

    tokens_all = lax.all_gather(tokens, "mp", axis=0, tiled=True)
    qkv_act, attn_low, log_sums = attention_block(tokens_all)
    branch = lax.psum_scatter(
        jnp.dot(attn_low, out_low, preferred_element_type=jnp.float32).astype(jnp.bfloat16),
        "mp",
        scatter_dimension=0,
        tiled=True,
    ).astype(jnp.float32)
    first, first_pull = jax.vjp(
        layer_norm, branch + norm_vectors[0] + tokens_wide, norm_vectors[2], norm_vectors[3]
    )
    first_low = first.astype(jnp.bfloat16)
    first_all = lax.all_gather(first_low, "mp", axis=0, tiled=True)
    pre, hidden = feed_block(first_all)
    ffn = lax.psum_scatter(
        jnp.dot(hidden, down_low, preferred_element_type=jnp.float32).astype(jnp.bfloat16),
        "mp",
        scatter_dimension=0,
        tiled=True,
    ).astype(jnp.float32)
    second, second_pull = jax.vjp(
        layer_norm, ffn + norm_vectors[1] + first, norm_vectors[4], norm_vectors[5]
    )
    layer_out = (second * valid_own).astype(jnp.bfloat16)
    d_second, d_gain_two, d_shift_two = second_pull(cotangent.astype(jnp.float32) * valid_own)
    d_ffn_low = d_second.astype(jnp.bfloat16)
    first_all = lax.all_gather(first_low, "mp", axis=0, tiled=True)
    pre, hidden = feed_block(first_all)
    d_ffn_all = lax.all_gather(d_ffn_low, "mp", axis=0, tiled=True)
    grad_down = jnp.einsum("tf,td->fd", hidden, d_ffn_all, preferred_element_type=jnp.float32)
    d_hidden = jnp.einsum("td,fd->tf", d_ffn_all, down_low, preferred_element_type=jnp.float32)
    gelu_value, gelu_pull = jax.vjp(partial(jax.nn.gelu, approximate=False), pre)
    d_pre = gelu_pull(d_hidden)[0].astype(jnp.bfloat16)
    grad_up = jnp.einsum("td,tf->df", first_all, d_pre, preferred_element_type=jnp.float32)
    grad_up_bias = jnp.sum(d_pre, axis=0, dtype=jnp.float32)
    d_first = (
        lax.psum_scatter(
            jnp.einsum("tf,df->td", d_pre, up_low, preferred_element_type=jnp.float32).astype(
                jnp.bfloat16
            ),
            "mp",
            scatter_dimension=0,
            tiled=True,
        ).astype(jnp.float32)
        + d_second
    )
    d_branch, d_gain_one, d_shift_one = first_pull(d_first)
    d_branch_low = d_branch.astype(jnp.bfloat16)
    tokens_all = lax.all_gather(tokens, "mp", axis=0, tiled=True)
    qkv_act, attn_low, log_sums = attention_block(tokens_all)
    d_branch_all = lax.all_gather(d_branch_low, "mp", axis=0, tiled=True)
    grad_out = jnp.einsum("te,td->ed", attn_low, d_branch_all, preferred_element_type=jnp.float32)
    d_attn = jnp.einsum(
        "td,ed->te", d_branch_all, out_low, preferred_element_type=jnp.float32
    ).astype(jnp.bfloat16)
    d_qkv = attend_backward(qkv_act, lengths, log_sums, d_attn).astype(jnp.bfloat16)
    grad_qkv = jnp.einsum("td,cte->cde", tokens_all, d_qkv, preferred_element_type=jnp.float32)
    grad_head_bias = jnp.stack(
        [jnp.sum(d_qkv[0], axis=0, dtype=jnp.float32), jnp.sum(d_qkv[2], axis=0, dtype=jnp.float32)]
    )
    tokens_grad = (
        lax.psum_scatter(
            jnp.einsum("cte,cde->td", d_qkv, qkv_low, preferred_element_type=jnp.float32).astype(
                jnp.bfloat16
            ),
            "mp",
            scatter_dimension=0,
            tiled=True,
        ).astype(jnp.float32)
        + d_branch
    )
    sum_qkv, sum_out, sum_up, sum_down = (
        lax.psum_scatter(grad_qkv, "dp", scatter_dimension=1, tiled=True),
        lax.psum_scatter(grad_out, "dp", scatter_dimension=1, tiled=True),
        lax.psum_scatter(grad_up, "dp", scatter_dimension=0, tiled=True),
        lax.psum_scatter(grad_down, "dp", scatter_dimension=1, tiled=True),
    )
    norm_part = jnp.stack(
        [
            jnp.sum(d_branch, axis=0),
            jnp.sum(d_second, axis=0),
            d_gain_one,
            d_shift_one,
            d_gain_two,
            d_shift_two,
        ]
    )
    head_full = lax.dynamic_update_slice_in_dim(
        jnp.zeros((2, head_width * model_size), jnp.float32),
        grad_head_bias,
        model_rank * head_width,
        1,
    )
    unit_full = lax.dynamic_update_slice_in_dim(
        jnp.zeros((unit_width * model_size,), jnp.float32), grad_up_bias, model_rank * unit_width, 0
    )
    sum_norm, head_total, unit_total = lax.psum((norm_part, head_full, unit_full), ("dp", "mp"))
    sum_head_bias = lax.dynamic_slice_in_dim(head_total, model_rank * head_width, head_width, 1)
    sum_up_bias = lax.dynamic_slice_in_dim(unit_total, model_rank * unit_width, unit_width, 0)
    divisor = math.sqrt(1000.0 * data_size * UTT)
    params = (qkv_weight, out_weight, up_weight, down_weight, head_bias, up_bias, norm_vectors)
    grad_list = (sum_qkv, sum_out, sum_up, sum_down, sum_head_bias, sum_up_bias, sum_norm)
    moments = (
        qkv_moment,
        out_moment,
        up_moment,
        down_moment,
        head_bias_moment,
        up_bias_moment,
        norm_moment,
    )
    averages = (
        qkv_average,
        out_average,
        up_average,
        down_average,
        head_bias_average,
        up_bias_average,
        norm_average,
    )
    nexts, moment_nexts, average_nexts = ([], [], [])
    for weight, grad, moment, average, scale_one in zip(
        params, grad_list, moments, averages, RATE_SCALES
    ):
        weight_next, moment_next, average_next = update_one(
            scale_one / divisor, weight, grad, moment, average
        )
        nexts.append(weight_next)
        moment_nexts.append(moment_next)
        average_nexts.append(average_next)
    return (
        layer_out,
        tokens_grad,
        grad_list[0],
        grad_list[1],
        grad_list[2],
        grad_list[3],
        grad_list[4],
        grad_list[5],
        grad_list[6],
        nexts[0],
        nexts[1],
        nexts[2],
        nexts[3],
        nexts[4],
        nexts[5],
        nexts[6],
        moment_nexts[0],
        moment_nexts[1],
        moment_nexts[2],
        moment_nexts[3],
        moment_nexts[4],
        moment_nexts[5],
        moment_nexts[6],
        average_nexts[0],
        average_nexts[1],
        average_nexts[2],
        average_nexts[3],
        average_nexts[4],
        average_nexts[5],
        average_nexts[6],
    )


def solution(mesh):
    return jax.shard_map(
        on_device,
        mesh=mesh,
        in_specs=(
            P(("dp", "mp"), None),
            P("dp", None),
            P(("dp", "mp"), None),
            P(None, "dp", "mp"),
            P("mp", "dp"),
            P("dp", "mp"),
            P("mp", "dp"),
            P(None, "mp"),
            P("mp"),
            P(),
            P(None, "dp", "mp"),
            P("mp", "dp"),
            P("dp", "mp"),
            P("mp", "dp"),
            P(None, "mp"),
            P("mp"),
            P(),
            P(None, "dp", "mp"),
            P("mp", "dp"),
            P("dp", "mp"),
            P("mp", "dp"),
            P(None, "mp"),
            P("mp"),
            P(),
        ),
        out_specs=(
            P(("dp", "mp"), None),
            P(("dp", "mp"), None),
            P(None, "dp", "mp"),
            P("mp", "dp"),
            P("dp", "mp"),
            P("mp", "dp"),
            P(None, "mp"),
            P("mp"),
            P(),
            P(None, "dp", "mp"),
            P("mp", "dp"),
            P("dp", "mp"),
            P("mp", "dp"),
            P(None, "mp"),
            P("mp"),
            P(),
            P(None, "dp", "mp"),
            P("mp", "dp"),
            P("dp", "mp"),
            P("mp", "dp"),
            P(None, "mp"),
            P("mp"),
            P(),
            P(None, "dp", "mp"),
            P("mp", "dp"),
            P("dp", "mp"),
            P("mp", "dp"),
            P(None, "mp"),
            P("mp"),
            P(),
        ),
        check_vma=False,
    )
```

profile of v0, /device:TPU:0, one launch (start us, length us, event | category | flops | bytes accessed | tf_op | source)
XLA Modules:
  0.0 702.4 jit_solution(5323415210953138753)
XLA Ops:
  14.4 34.9 %all_gather.28 = bf16[192,768]{0,1:T(8,128)(2,1)} all-gather(bf16[192,96]{0,1:T(8,128)(2,1)S(1)} %copy.103), channel_id=1, replica_groups=mesh['dp'=8,'mp'=4] {'dp'}, dimensions={1}, use_global_device_ids=true | all-gather | bytes 331776 | tf_op jit(solution)/shard_map/all_gather | solution.py:140
  50.1 38.1 %all_gather.26 = bf16[3,768,192]{2,0,1:T(4,128)(2,1)S(1)} all-gather(bf16[3,96,192]{2,0,1:T(4,128)(2,1)S(1)} %copy.98), channel_id=1, replica_groups=mesh['dp'=8,'mp'=4] {'dp'}, dimensions={1}, use_global_device_ids=true | all-gather | bytes 995328 | tf_op jit(solution)/shard_map/all_gather | solution.py:139
  109.7 30.6 %reduce-scatter.13.cloned.1.call-done = bf16[416,768]{1,0:T(8,128)(2,1)} async-done(((bf16[1664,768]{1,0:T(8,128)(2,1)}), bf16[416,768]{1,0:T(8,128)(2,1)}) %reduce-scatter.13.cloned.1.call-update) | async-done | bytes 638992 | tf_op jit(solution)/shard_map/reduce_scatter | solution.py:166
  150.8 25.4 %all-gather.9.cloned.1.call-done = bf16[1664,768]{1,0:T(8,128)(2,1)} async-done(((bf16[416,768]{1,0:T(8,128)(2,1)}), bf16[1664,768]{1,0:T(8,128)(2,1)}) %all-gather.9.cloned.1.call-update) | async-done | bytes 2555920 | tf_op jit(solution)/shard_map/all_gather | solution.py:176
  176.2 16.3 %multiply_convert_fusion.1 = (bf16[1664,768]{1,0:T(8,128)(2,1)}, f32[1664,768]{1,0:T(8,128)}, f32[1664,768]{1,0:T(8,128)}) fusion(f32[768]{0:T(1024)} %param.32, bf16[1664,768]{1,0:T(8,128)(2,1)} %all-gather.9.cloned.1.call-done, bf16[768,768]{1,0:T(8,128)(2,1)} %all-gather.11.cloned.1.call-done), kind=kOutput, calls=%fused_computation.13 | convolution fusion | flops 2047279104 | bytes 16518144 | tf_op jit(solution)/shard_map/dot_general | solution.py:161
  192.5 27.7 %all-gather.13.cloned.1.call-done = bf16[768,768]{0,1:T(8,128)(2,1)} async-done(((bf16[768,96]{0,1:T(8,128)(2,1)}), bf16[768,768]{0,1:T(8,128)(2,1)}) %all-gather.13.cloned.1.call-update) | async-done | bytes 1179664 | tf_op jit(solution)/shard_map/all_gather | solution.py:142
  220.2 5.7 convolution_convert_fusion.1
  227.3 31.0 %reduce-scatter.15.cloned.1.call-done = bf16[416,768]{1,0:T(8,128)(2,1)} async-done(((bf16[1664,768]{1,0:T(8,128)(2,1)}), bf16[416,768]{1,0:T(8,128)(2,1)}) %reduce-scatter.15.cloned.1.call-update) | async-done | bytes 638992 | tf_op jit(solution)/shard_map/reduce_scatter | solution.py:178
  266.6 25.1 %all-gather.15.cloned.1.call-done = bf16[1664,768]{1,0:T(8,128)(2,1)} async-done(((bf16[416,768]{1,0:T(8,128)(2,1)}), bf16[1664,768]{1,0:T(8,128)(2,1)}) %all-gather.15.cloned.1.call-update) | async-done | bytes 2555920 | tf_op jit(solution)/shard_map/all_gather | solution.py:192
  291.7 9.4 %convert_reduce_fusion = (f32[768]{0:T(1024)}, bf16[1664,768]{1,0:T(8,128)(2,1)S(1)}) fusion(f32[1664,768]{1,0:T(8,128)} %get-tuple-element.169, f32[1664,768]{1,0:T(8,128)} %get-tuple-element.194, f32[768]{0:T(1024)} %param.32, bf16[1664,768]{1,0:T(8,128)(2,1)} %all-gather.15.cloned.1.call-done, bf16[768,768]{0,1:T(8,128)(2,1)} %all-gather.13.cloned.1.call-done), kind=kOutput, calls=%fused_computation.11 | convolution fusion | flops 1984658688 | bytes 16521216 | tf_op jit(solution)/shard_map/td,fd->tf/dot_general | solution.py:194
  306.4 34.1 %reduce-scatter.17.cloned.1.call-done = bf16[416,768]{1,0:T(8,128)(2,1)} async-done(((bf16[1664,768]{1,0:T(8,128)(2,1)}), bf16[416,768]{1,0:T(8,128)(2,1)}) %reduce-scatter.17.cloned.1.call-update) | async-done | bytes 638992 | tf_op jit(solution)/shard_map/reduce_scatter | solution.py:200
  349.1 6.2 fusion.72
  357.5 6.3 fusion.71
  364.1 10.1 %all-gather.17.cloned.1.call-done = bf16[1664,768]{1,0:T(8,128)(2,1)} async-done(((bf16[416,768]{1,0:T(8,128)(2,1)}), bf16[1664,768]{1,0:T(8,128)(2,1)}) %all-gather.17.cloned.1.call-update) | async-done | bytes 2555920 | tf_op jit(solution)/shard_map/all_gather | solution.py:214
  388.5 9.2 %multiply_reduce_fusion = (f32[3,896]{1,0:T(4,128)S(1)}, f32[3,896,896]{1,2,0:T(8,128)}) fusion(f32[3,896,896]{1,2,0:T(8,128)} %copy-done, f32[3,896]{1,0:T(4,128)S(1)} %log_add_fusion, bf16[896,3,64]{0,2,1:T(8,128)(2,1)S(1)} %bitcast.150, bf16[896,3,64]{0,2,1:T(8,128)(2,1)S(1)} %bitcast.168), kind=kOutput, calls=%fused_computation.1 | convolution fusion | flops 315504000 | bytes 19977216 | tf_op jit(solution)/shard_map/uqhd,ukhd->uhqk/dot_general | solution.py:85
  397.7 10.7 %multiply_convert_fusion = bf16[3,896,896]{1,2,0:T(8,128)(2,1)} fusion(f32[3,896,896]{1,2,0:T(8,128)} %get-tuple-element.196, f32[3,896,896]{1,2,0:T(8,128)} %copy-done, f32[3,896]{1,0:T(4,128)S(1)} %get-tuple-element.195, f32[3,896]{1,0:T(4,128)S(1)} %log_add_fusion), kind=kLoop, calls=%fused_computation | loop fusion | flops 9633792 | bytes 24105984 | tf_op jit(solution)/shard_map/convert_element_type | solution.py:89
  411.9 5.5 fusion.30
  431.9 5.8 bitcast_convert_fusion
  440.7 7.3 %reduce-scatter.23.cloned.1.call-done = f32[768,96]{0,1:T(8,128)} async-done(((f32[768,768]{0,1:T(8,128)}), f32[768,96]{0,1:T(8,128)}) %reduce-scatter.23.cloned.1.call-update) | async-done | bytes 294928 | tf_op jit(solution)/shard_map/reduce_scatter | solution.py:239
  450.2 71.0 %reduce-scatter.21.cloned.1.call-done = f32[96,768]{1,0:T(8,128)} async-done(((f32[768,768]{1,0:T(8,128)}), f32[96,768]{1,0:T(8,128)}) %reduce-scatter.21.cloned.1.call-update) | async-done | bytes 294928 | tf_op jit(solution)/shard_map/reduce_scatter | solution.py:238
  523.9 40.9 %all-reduce = (f32[2,768]{1,0:T(2,128)S(1)}, f32[3072]{0:T(1024)S(1)}, f32[6,768]{1,0:T(8,128)S(1)}) all-reduce(f32[2,768]{1,0:T(2,128)S(1)} %dynamic_update_slice.6, f32[3072]{0:T(1024)S(1)} %dynamic_update_slice.7, f32[6,768]{1,0:T(8,128)S(1)} %stack.80), channel_id=1, replica_groups=mesh['dp'=8,'mp'=4] {'dp','mp'}, use_global_device_ids=true, to_apply=%region_27.28 | all-reduce | flops 9216 | bytes 73728 | tf_op jit(solution)/shard_map/psum | solution.py:260
  566.9 20.0 %reduce-scatter.27.cloned.1.call-done = f32[96,192]{1,0:T(8,128)} async-done(((f32[768,192]{1,0:T(8,128)}), f32[96,192]{1,0:T(8,128)}) %reduce-scatter.27.cloned.1.call-update) | async-done | bytes 73744
  588.7 68.1 %reduce-scatter.25.cloned.1.call-done = f32[96,576]{1,0:T(8,128)} async-done(((f32[768,576]{1,0:T(8,128)}), f32[96,576]{1,0:T(8,128)}) %reduce-scatter.25.cloned.1.call-update) | async-done | bytes 221200
  661.7 30.8 %reduce-scatter.19.cloned.1.call-done = bf16[416,768]{1,0:T(8,128)(2,1)} async-done(((bf16[1664,768]{1,0:T(8,128)(2,1)}), bf16[416,768]{1,0:T(8,128)(2,1)}) %reduce-scatter.19.cloned.1.call-update) | async-done | bytes 638992 | tf_op jit(solution)/shard_map/reduce_scatter | solution.py:225
  (346 shorter events, 114.8 us)
Async XLA Ops:
  8.0 80.1 %all-gather.7.cloned.1.call-start = ((), (), s32[]{:S(2)}) async-start(), calls=%async_computation.8 | async-start | bytes 3194880 | tf_op jit(solution)/shard_map/all_gather | solution.py:164
  8.8 131.5 %reduce-scatter.13.cloned.1.call-start = ((), (), s32[]{:S(2)}) async-start(), calls=%async_computation.9 | async-start | bytes 3194880 | tf_op jit(solution)/shard_map/reduce_scatter | solution.py:166
  106.8 43.9 %all-gather.11.cloned.1.call-start = ((), (), s32[]{:S(2)}) async-start(), calls=%async_computation.11 | async-start | bytes 1327104 | tf_op jit(solution)/shard_map/all_gather | solution.py:141
  108.5 67.6 %all-gather.9.cloned.1.call-start = ((), (), s32[]{:S(2)}) async-start(), calls=%async_computation.10 | async-start | bytes 3194880 | tf_op jit(solution)/shard_map/all_gather | solution.py:176
  145.5 74.7 %all-gather.13.cloned.1.call-start = ((), (), s32[]{:S(2)}) async-start(), calls=%async_computation.12 | async-start | bytes 1327104 | tf_op jit(solution)/shard_map/all_gather | solution.py:142
  147.2 111.2 %reduce-scatter.15.cloned.1.call-start = ((), (), s32[]{:S(2)}) async-start(), calls=%async_computation.13 | async-start | bytes 3194880 | tf_op jit(solution)/shard_map/reduce_scatter | solution.py:178
  225.9 65.8 %all-gather.15.cloned.1.call-start = ((), (), s32[]{:S(2)}) async-start(), calls=%async_computation.14 | async-start | bytes 3194880 | tf_op jit(solution)/shard_map/all_gather | solution.py:192
  266.4 74.1 %reduce-scatter.17.cloned.1.call-start = ((), (), s32[]{:S(2)}) async-start(), calls=%async_computation.15 | async-start | bytes 3194880 | tf_op jit(solution)/shard_map/reduce_scatter | solution.py:200
  306.3 67.8 %all-gather.17.cloned.1.call-start = ((), (), s32[]{:S(2)}) async-start(), calls=%async_computation.16 | async-start | bytes 3194880 | tf_op jit(solution)/shard_map/all_gather | solution.py:214
  349.0 98.9 %reduce-scatter.23.cloned.1.call-start = ((), (), s32[]{:S(2)}) async-start(), calls=%async_computation.19 | async-start | bytes 2654208 | tf_op jit(solution)/shard_map/reduce_scatter | solution.py:239
  355.3 165.9 %reduce-scatter.21.cloned.1.call-start = ((), (), s32[]{:S(2)}) async-start(), calls=%async_computation.18 | async-start | bytes 2654208 | tf_op jit(solution)/shard_map/reduce_scatter | solution.py:238
  363.8 223.1 %reduce-scatter.27.cloned.1.call-start = ((), (), s32[]{:S(2)}) async-start(), calls=%async_computation.21 | async-start | bytes 884736
  417.5 239.4 %reduce-scatter.25.cloned.1.call-start = ((), (), s32[]{:S(2)}) async-start(), calls=%async_computation.20 | async-start | bytes 2211840
  431.8 260.7 %reduce-scatter.19.cloned.1.call-start = ((), (), s32[]{:S(2)}) async-start(), calls=%async_computation.17 | async-start | bytes 3194880 | tf_op jit(solution)/shard_map/reduce_scatter | solution.py:225
  450.1 114.9 %copy-start.96 = (f32[2,192]{1,0:T(2,128)S(1)}, f32[2,192]{1,0:T(2,128)}, u32[]{:S(2)}) copy-start(f32[2,192]{1,0:T(2,128)} %param.45) | copy-start | bytes 4612
  450.1 114.9 %copy-start.97 = (f32[2,192]{1,0:T(2,128)S(1)}, f32[2,192]{1,0:T(2,128)}, u32[]{:S(2)}) copy-start(f32[2,192]{1,0:T(2,128)} %param.38) | copy-start | bytes 4612
  450.1 115.5 %copy-start.92 = (f32[768]{0:T(1024)S(1)}, f32[768]{0:T(1024)}, u32[]{:S(2)}) copy-start(f32[768]{0:T(1024)} %param.32) | copy-start | bytes 9220
  450.1 115.5 %copy-start.93 = (f32[768]{0:T(1024)S(1)}, f32[768]{0:T(1024)}, u32[]{:S(2)}) copy-start(f32[768]{0:T(1024)} %param.46) | copy-start | bytes 9220
  450.1 115.5 %copy-start.94 = (f32[768]{0:T(1024)S(1)}, f32[768]{0:T(1024)}, u32[]{:S(2)}) copy-start(f32[768]{0:T(1024)} %param.39) | copy-start | bytes 9220
  450.1 116.2 %copy-start.73 = (f32[6,768]{1,0:T(8,128)S(1)}, f32[6,768]{1,0:T(8,128)}, u32[]{:S(2)}) copy-start(f32[6,768]{1,0:T(8,128)} %param.47) | copy-start | bytes 55300
  450.1 116.2 %copy-start.74 = (f32[6,768]{1,0:T(8,128)S(1)}, f32[6,768]{1,0:T(8,128)}, u32[]{:S(2)}) copy-start(f32[6,768]{1,0:T(8,128)} %param.40) | copy-start | bytes 55300
  450.1 137.8 %copy-start.59 = (f32[192,96]{1,0:T(8,128)S(1)}, f32[192,96]{1,0:T(8,128)}, u32[]{:S(2)}) copy-start(f32[192,96]{1,0:T(8,128)} %param.28) | copy-start | bytes 221188
  450.1 137.8 %copy-start.62 = (f32[192,96]{1,0:T(8,128)S(1)}, f32[192,96]{1,0:T(8,128)}, u32[]{:S(2)}) copy-start(f32[192,96]{1,0:T(8,128)} %param.42) | copy-start | bytes 221188
  450.1 137.8 %copy-start.63 = (f32[192,96]{1,0:T(8,128)S(1)}, f32[192,96]{1,0:T(8,128)}, u32[]{:S(2)}) copy-start(f32[192,96]{1,0:T(8,128)} %param.35) | copy-start | bytes 221188
  (97 other events, 1965.9 us)
Sparse Core Ops, SparseCore 0:
  10.4 27.8 all-gather.6
  106.9 33.3 reduce-scatter.12
  266.5 25.1 all-gather.14
  306.5 34.0 reduce-scatter.16
Sparse Core Ops, SparseCore 1:
  110.1 40.6 all-gather.10
  152.8 23.4 all-gather.8
  178.8 41.3 all-gather.12
  226.0 32.3 reduce-scatter.14
  349.1 25.0 all-gather.16
  378.2 69.7 reduce-scatter.22
  451.9 69.2 reduce-scatter.20
  524.4 62.5 reduce-scatter.26
  590.3 66.5 reduce-scatter.24
  659.5 32.9 reduce-scatter.18
where the time goes:
time: 711 us; the launch traced here: 702 us
  waiting for transfers between devices  386 us (54%)
  blocking collectives  114 us (16%)
  matrix products  104 us (15%)
  other arithmetic  51.8 us (7%)
  local copies, waits for them, and re-layouts  28.2 us (4%)
  between operations  17.2 us (2%)
    unnamed x16, waiting for transfers between devices  89 us
    reduce_scatter x1, waiting for transfers between devices, on_device(): lax.psum_scatter(grad_up, 'dp', scatter_dimension=0, tiled=True)  71 us
    psum x1, blocking collectives, on_device(): lax.psum((norm_part, head_full, unit_full), ('dp', 'mp'))  40.9 us
    all_gather x1, blocking collectives, on_device(): lax.all_gather(qkv_weight.astype(jnp.bfloat16), 'dp', axis=1, tiled=True)  38.1 us
    all_gather x1, blocking collectives, on_device(): lax.all_gather(out_weight.astype(jnp.bfloat16), 'dp', axis=1, tiled=True)  34.9 us
    reduce_scatter x1, waiting for transfers between devices, on_device(): lax.psum_scatter(jnp.einsum('tf,df->td', d_pre, up_low, preferred_element...  34.1 us
    reduce_scatter x1, waiting for transfers between devices, on_device(): lax.psum_scatter(jnp.dot(hidden, down_low, preferred_element_type=jnp.flo...  31 us
    reduce_scatter x1, waiting for transfers between devices, on_device(): lax.psum_scatter(jnp.einsum('cte,cde->td', d_qkv, qkv_low, preferred_elem...  30.8 us
  transfers between devices with their start and end apart: 14, of which 13 were waited for; matrix products, arithmetic and copies ran while one was open for 18% of the time, Pallas kernels for 0%

commit v1 on v0

v1 whole, which is shorter than its diff:
```python
import math

import jax
import jax.numpy as jnp
from jax import lax
from jax.sharding import PartitionSpec as P

HEAD_DIM = 64
UTT = 1
LENS = (256, 512, 896)
MOSTS = (200, 400, 781)

EPS = 1e-05
MOMENTUM = 0.5
DECAY = 0.5
RATE_SCALES = (0.02, 0.16, 0.02, 0.02, 0.02, 0.32, 0.16)
NEG_FILL = -1000000000.0
BF16 = jnp.bfloat16
F32 = jnp.float32


def dot(a, b, dims):
    return lax.dot_general(a, b, (dims, ((), ())), preferred_element_type=F32)


CORE_SWAP = [(0, 1), (1, 0), (2, 3), (3, 2)]
HALF_SWAP = [(0, 2), (2, 0), (1, 3), (3, 1)]


def core_swap(value):
    return lax.ppermute(value, "mp", CORE_SWAP)


def half_swap(value):
    return lax.ppermute(value, "mp", HALF_SWAP)


def dp_dims(size):
    dims = []
    while size % 4 == 0:
        dims.append(4)
        size //= 4
    if size > 1:
        dims.append(size)
    return tuple(dims)


class Grid:
    def __init__(self, size):
        self.dims = dp_dims(size)
        self.size = size
        rank = lax.axis_index("dp")
        self.strides = []
        stride = size
        for extent in self.dims:
            stride //= extent
            self.strides.append(stride)
        self.coords = [lax.rem(rank // s, e) for s, e in zip(self.strides, self.dims)]

    def send(self, value, stage, ahead):
        extent, stride = self.dims[stage], self.strides[stage]
        pairs = []
        for source in range(self.size):
            at = source // stride % extent
            pairs.append((source, source + ((at + ahead) % extent - at) * stride))
        return lax.ppermute(value, "dp", pairs)


def put(buffer, piece, axis, index):
    starts = [0] * buffer.ndim
    starts[axis] = index
    return lax.dynamic_update_slice(buffer, jnp.expand_dims(piece, axis), tuple(starts))


def take(buffer, axis, index):
    return lax.dynamic_index_in_dim(buffer, index, axis, keepdims=False)


def gather_half(grid, shard, half_stage):
    rows, columns = shard.shape
    value = shard[None]
    done = 0
    order = list(range(len(grid.dims)))
    for stage in order:
        if done == half_stage:
            value = jnp.concatenate([value, half_swap(value)], 0)
        extent, coord = grid.dims[stage], grid.coords[stage]
        axis = 1 + done
        shape = value.shape[:axis] + (extent,) + value.shape[axis:]
        buffer = put(jnp.zeros(shape, value.dtype), value, axis, coord)
        for ahead in range(1, extent):
            source = lax.rem(coord + extent - ahead, extent)
            buffer = put(buffer, grid.send(value, stage, ahead), axis, source)
        value = buffer
        done += 1
    if done == half_stage:
        other = half_swap(value)
        return value.reshape(-1, columns), other.reshape(-1, columns)
    return value[0].reshape(-1, columns), value[1].reshape(-1, columns)


def scatter_sum(grid, mine, theirs, half_first):
    columns = mine.shape[1]
    shape = grid.dims + (mine.shape[0] // grid.size, columns)
    order = list(range(len(grid.dims)))[::-1]

    def along(value, stage):
        extent, coord = grid.dims[stage], grid.coords[stage]
        axis = value.ndim - 3
        total = take(value, axis, coord).astype(F32)
        for ahead in range(1, extent):
            piece = take(value, axis, lax.rem(coord + ahead, extent))
            total = total + grid.send(piece.astype(BF16), stage, ahead).astype(F32)
        return total

    mine, theirs = mine.reshape(shape), theirs.reshape(shape)
    if half_first:
        value = mine.astype(F32) + half_swap(theirs.astype(BF16)).astype(F32)
        for stage in order:
            value = along(value, stage)
        return value
    first = order[0]
    mine = along(mine, first)
    theirs = along(theirs, first)
    value = mine + half_swap(theirs.astype(BF16)).astype(F32)
    for stage in order[1:]:
        value = along(value, stage)
    return value


def sum_all(grid, value, over_cores):
    for stage in range(len(grid.dims)):
        total = value
        for ahead in range(1, grid.dims[stage]):
            total = total + grid.send(value, stage, ahead)
        value = total
    value = value + half_swap(value)
    if over_cores:
        value = value + core_swap(value)
    return value


def offsets():
    listing, offset = [], 0
    for extent in LENS:
        listing.append(offset)
        offset += UTT * extent
    return listing


def move_plan(rows_local):
    start = offsets()[2]
    count = 2 * rows_local - start
    free = -(-(start + MOSTS[2] - 3 * rows_local) // 16) * 16
    return rows_local - count, free, count


def row_table(rows_local, member, lengths):
    source, free, count = move_plan(rows_local)
    starts = offsets()
    local = jnp.arange(rows_local)
    row = member * rows_local + local
    slot = (row >= starts[1]).astype(jnp.int32) + (row >= starts[2]).astype(jnp.int32)
    place = row - jnp.where(slot == 0, starts[0], jnp.where(slot == 1, starts[1], starts[2]))
    arrived = (member == 3) & (local >= free) & (local < free + count)
    left = (member == 1) & (local >= source)
    place = jnp.where(arrived, local - free, place)
    length = jnp.where(slot == 0, lengths[0, 0], jnp.where(slot == 1, lengths[0, 1], lengths[0, 2]))
    return slot, (place < length) & ~left


def bring(rows, member):
    source, free, count = move_plan(rows.shape[0])
    moved = lax.ppermute(rows[source:], "mp", [(1, 3)])
    placed = lax.dynamic_update_slice(rows, moved, (free, 0))
    return jnp.where(member == 3, placed, rows)


def send_back(rows, member):
    source, free, count = move_plan(rows.shape[0])
    moved = lax.ppermute(rows[free : free + count], "mp", [(3, 1)])
    placed = lax.dynamic_update_slice(rows, moved, (source, 0))
    cleared = lax.dynamic_update_slice(rows, jnp.zeros_like(moved), (free, 0))
    return jnp.where(member == 1, placed, jnp.where(member == 3, cleared, rows))


def norm_stats(values):
    mean = jnp.mean(values, axis=-1, keepdims=True)
    center = values - mean
    spread = jnp.mean(center * center, axis=-1, keepdims=True)
    inverse = lax.rsqrt(spread + EPS)
    return center * inverse, inverse


def norm_back(grad, unit, inverse, gain):
    scaled = grad * gain
    return inverse * (
        scaled
        - jnp.mean(scaled, axis=-1, keepdims=True)
        - unit * jnp.mean(scaled * unit, axis=-1, keepdims=True)
    )


def attend(query, keys, values, allowed):
    scores = jnp.einsum("qhd,khd->hqk", query, keys, preferred_element_type=F32)
    scores = jnp.where(allowed[None], scores * HEAD_DIM ** (-0.5), NEG_FILL)
    peak = jnp.max(scores, axis=-1, keepdims=True)
    weights = jnp.exp(scores - peak)
    total = jnp.sum(weights, axis=-1, keepdims=True)
    low = (weights / total).astype(BF16)
    out = jnp.einsum("hqk,khd->qhd", low, values, preferred_element_type=F32)
    return out.astype(BF16), peak + jnp.log(total)


def attend_back(query, keys, values, allowed, log_sum, grad):
    scale = HEAD_DIM ** (-0.5)
    scores = jnp.einsum("qhd,khd->hqk", query, keys, preferred_element_type=F32)
    scores = jnp.where(allowed[None], scores * scale, NEG_FILL)
    probs = jnp.exp(scores - log_sum)
    d_values = jnp.einsum("hqk,qhd->khd", probs.astype(BF16), grad, preferred_element_type=F32)
    d_probs = jnp.einsum("qhd,khd->hqk", grad, values, preferred_element_type=F32)
    mean = jnp.sum(probs * d_probs, axis=-1, keepdims=True)
    low = (probs * (d_probs - mean)).astype(BF16)
    d_query = jnp.einsum("hqk,khd->qhd", low, keys, preferred_element_type=F32) * scale
    d_keys = jnp.einsum("hqk,qhd->khd", low, query, preferred_element_type=F32) * scale
    return d_query.astype(BF16), d_keys.astype(BF16), d_values.astype(BF16)


def update_one(rate, weight, grad, moment, average):
    moment_next = MOMENTUM * moment + grad
    weight_next = weight - rate * (grad + MOMENTUM * moment_next)
    return (weight_next, moment_next, DECAY * average + (1.0 - DECAY) * weight_next)


def on_device(
    tokens,
    lengths,
    cotangent,
    qkv_weight,
    out_weight,
    up_weight,
    down_weight,
    head_bias,
    up_bias,
    norm_vectors,
    qkv_moment,
    out_moment,
    up_moment,
    down_moment,
    head_bias_moment,
    up_bias_moment,
    norm_moment,
    qkv_average,
    out_average,
    up_average,
    down_average,
    head_bias_average,
    up_bias_average,
    norm_average,
):
    grid = Grid(lax.axis_size("dp"))
    member = lax.axis_index("mp")
    mate = member + 1 - 2 * lax.rem(member, 2)
    rows_local, width = tokens.shape
    head_width = qkv_weight.shape[2]
    stages = len(grid.dims)

    qkv_shard = jnp.transpose(qkv_weight, (1, 0, 2)).reshape(-1, 3 * head_width).astype(BF16)
    qkv_pair = gather_half(grid, qkv_shard, stages)
    out_pair = gather_half(grid, out_weight.astype(BF16).T, stages - 1)
    up_pair = gather_half(grid, up_weight.astype(BF16), stages)
    down_pair = gather_half(grid, down_weight.astype(BF16).T, stages - 1)
    bias_pair = (head_bias, half_swap(head_bias))
    up_bias_pair = (up_bias, half_swap(up_bias))

    slot_own, valid_own = row_table(rows_local, member, lengths)
    slot_mate, valid_mate = row_table(rows_local, mate, lengths)
    slot = jnp.concatenate([slot_own, slot_mate])
    frame = jnp.concatenate([valid_own, valid_mate])
    allowed = (slot[:, None] == slot[None, :]) & frame[None, :]
    live = valid_own[:, None]

    def share(rows):
        return jnp.concatenate([rows, core_swap(rows)], 0)

    def settle(partial):
        return partial[:rows_local] + core_swap(partial[rows_local:].astype(BF16)).astype(F32)

    own_tokens = bring(tokens, member)
    own_cotangent = bring(cotangent, member)
    tokens_all = share(own_tokens)

    heads = 2 * head_width // HEAD_DIM
    parts = []
    for weight, bias in zip(qkv_pair, bias_pair):
        rows_bias = jnp.concatenate([bias[0], jnp.zeros_like(bias[0]), bias[1]])
        act = (dot(tokens_all, weight, ((1,), (0,))) + rows_bias).astype(BF16)
        parts.append(act.reshape(2 * rows_local, 3, -1, HEAD_DIM))
    act = jnp.concatenate(parts, 2)
    query, keys, values = act[:, 0], act[:, 1], act[:, 2]
    attn, log_sum = attend(query, keys, values, allowed)
    attn = attn.reshape(2 * rows_local, -1)
    out_both = jnp.concatenate(out_pair, 1)
    branch = settle(dot(attn, out_both, ((1,), (1,))))
    unit_one, inverse_one = norm_stats(branch + norm_vectors[0] + own_tokens.astype(F32))
    first = unit_one * norm_vectors[2] + norm_vectors[3]
    first_all = share(first.astype(BF16))

    up_both = jnp.concatenate(up_pair, 1)
    down_both = jnp.concatenate(down_pair, 1)
    pre = dot(first_all, up_both, ((1,), (0,))) + jnp.concatenate(up_bias_pair)
    phi = 0.5 * (1.0 + lax.erf(pre * (0.5**0.5)))
    density = jnp.exp(-0.5 * pre * pre) * (1.0 / math.sqrt(2.0 * math.pi))
    hidden = (pre * phi).astype(BF16)
    slope = (phi + pre * density).astype(BF16)
    ffn = settle(dot(hidden, down_both, ((1,), (1,))))
    unit_two, inverse_two = norm_stats(ffn + norm_vectors[1] + first)
    second = unit_two * norm_vectors[4] + norm_vectors[5]
    layer_out = send_back(jnp.where(live, second, 0.0).astype(BF16), member)

    grad_two = jnp.where(live, own_cotangent.astype(F32), 0.0)
    d_second = norm_back(grad_two, unit_two, inverse_two, norm_vectors[4])
    d_ffn_all = share(d_second.astype(BF16))
    d_hidden = dot(d_ffn_all, down_both, ((1,), (0,)))
    d_pre = (d_hidden * slope.astype(F32)).astype(BF16)
    d_first = settle(dot(d_pre, up_both, ((1,), (1,)))) + d_second
    units = up_weight.shape[1]
    grad_down = [
        dot(d_ffn_all, hidden[:, at : at + units], ((0,), (0,))).astype(BF16) for at in (0, units)
    ]
    sum_down = scatter_sum(grid, *grad_down, True).T
    grad_up = [
        dot(first_all, d_pre[:, at : at + units], ((0,), (0,))).astype(BF16) for at in (0, units)
    ]
    sum_up = scatter_sum(grid, *grad_up, False)
    grad_up_bias = jnp.sum(d_pre, axis=0, dtype=F32)

    d_branch = norm_back(d_first, unit_one, inverse_one, norm_vectors[2])
    d_branch_all = share(d_branch.astype(BF16))
    d_attn = dot(d_branch_all, out_both, ((1,), (0,))).astype(BF16)
    grad_out = [
        dot(d_branch_all, attn[:, at : at + head_width], ((0,), (0,))).astype(BF16)
        for at in (0, head_width)
    ]
    sum_out = scatter_sum(grid, *grad_out, True).T
    d_query, d_keys, d_values = attend_back(
        query, keys, values, allowed, log_sum, d_attn.reshape(2 * rows_local, heads, HEAD_DIM)
    )
    half_heads = heads // 2
    d_parts = []
    for at in (0, half_heads):
        d_parts.append(
            jnp.concatenate(
                [
                    piece[:, at : at + half_heads].reshape(2 * rows_local, -1)
                    for piece in (d_query, d_keys, d_values)
                ],
                1,
            )
        )
    grad_qkv = [dot(tokens_all, part, ((0,), (0,))).astype(BF16) for part in d_parts]
    sum_qkv = scatter_sum(grid, *grad_qkv, True)
    sum_qkv = jnp.transpose(sum_qkv.reshape(-1, 3, head_width), (1, 0, 2))
    grad_bias = [jnp.sum(part, axis=0, dtype=F32) for part in d_parts]
    d_tokens = settle(
        dot(d_parts[0], qkv_pair[0], ((1,), (1,))) + dot(d_parts[1], qkv_pair[1], ((1,), (1,)))
    )
    tokens_grad = send_back(d_tokens + d_branch, member)

    norm_part = jnp.stack(
        [
            jnp.sum(d_branch, axis=0),
            jnp.sum(d_second, axis=0),
            jnp.sum(d_first * unit_one, axis=0),
            jnp.sum(d_first, axis=0),
            jnp.sum(grad_two * unit_two, axis=0),
            jnp.sum(grad_two, axis=0),
        ]
    )
    sum_norm = sum_all(grid, norm_part, True)

    def sum_half(pair):
        value = pair[0] + half_swap(pair[1])
        for stage in range(stages):
            total = value
            for ahead in range(1, grid.dims[stage]):
                total = total + grid.send(value, stage, ahead)
            value = total
        return value

    sum_up_bias = sum_half((grad_up_bias[:units], grad_up_bias[units:]))
    sum_bias = sum_half(grad_bias)
    sum_head_bias = jnp.stack([sum_bias[:head_width], sum_bias[2 * head_width :]])

    divisor = math.sqrt(1000.0 * grid.size * UTT)
    params = (qkv_weight, out_weight, up_weight, down_weight, head_bias, up_bias, norm_vectors)
    grads = (sum_qkv, sum_out, sum_up, sum_down, sum_head_bias, sum_up_bias, sum_norm)
    moments = (
        qkv_moment,
        out_moment,
        up_moment,
        down_moment,
        head_bias_moment,
        up_bias_moment,
        norm_moment,
    )
    averages = (
        qkv_average,
        out_average,
        up_average,
        down_average,
        head_bias_average,
        up_bias_average,
        norm_average,
    )
    nexts, moment_nexts, average_nexts = ([], [], [])
    for weight, grad, moment, average, scale_one in zip(
        params, grads, moments, averages, RATE_SCALES
    ):
        weight_next, moment_next, average_next = update_one(
            scale_one / divisor, weight, grad, moment, average
        )
        nexts.append(weight_next)
        moment_nexts.append(moment_next)
        average_nexts.append(average_next)
    return (layer_out, tokens_grad, *grads, *nexts, *moment_nexts, *average_nexts)


ROWS = P(("dp", "mp"), None)
PARAMS = (
    P(None, "dp", "mp"),
    P("mp", "dp"),
    P("dp", "mp"),
    P("mp", "dp"),
    P(None, "mp"),
    P("mp"),
    P(),
)


def solution(mesh):
    return jax.shard_map(
        on_device,
        mesh=mesh,
        in_specs=(ROWS, P("dp", None), ROWS) + PARAMS * 3,
        out_specs=(ROWS, ROWS) + PARAMS * 4,
        check_vma=False,
    )
```

time: 711 us -> 464 us (0.65)
  waiting for transfers between devices: 386 us -> 122 us
  blocking collectives: 114 us -> 0 us
  starting transfers between devices: 1.7 us -> 93.2 us
  local copies, waits for them, and re-layouts: 28.2 us -> 97 us
  matrix products: 104 us -> 87.1 us
  between operations: 17.2 us -> 2.74 us
    reduce_scatter x6 -> x0, waiting for transfers between devices: 205 us -> none  [the longest x1 71 us: on_device(): lax.psum_scatter(grad_up, 'dp', scatter_dimension=0, tiled=True)]
    ppermute x0 -> x71, waiting for transfers between devices: none -> 122 us  [the longest x45 86.2 us: send(): return lax.ppermute(value, 'dp', pairs)]
    ppermute x0 -> x71, starting transfers between devices: none -> 93.2 us  [the longest x45 67.7 us: send(): return lax.ppermute(value, 'dp', pairs)]
    all_gather x6 -> x0, waiting for transfers between devices: 91.8 us -> none  [the longest x1 27.7 us: on_device(): lax.all_gather(down_weight.astype(jnp.bfloat16), 'dp', axis=1, tiled=True)]
    unnamed x16 -> x0, waiting for transfers between devices: 89 us -> none
    all_gather x2 -> x0, blocking collectives: 72.9 us -> none  [the longest x1 38.1 us: on_device(): lax.all_gather(qkv_weight.astype(jnp.bfloat16), 'dp', axis=1, tiled=True)]
    dynamic_update_slice x2 -> x23, local copies, waits for them, and re-layouts: 0.47 us -> 46.2 us  [the longest x21 46.2 us: put(): lax.dynamic_update_slice(buffer, jnp.expand_dims(piece, axis), tuple(star...]
    psum x1 -> x0, blocking collectives: 40.9 us -> none  [on_device(): lax.psum((norm_part, head_full, unit_full), ('dp', 'mp'))]
  transfers between devices with their start and end apart: 14 -> 71, of which waited for: 13 -> 15; matrix products, arithmetic and copies ran while one was open for 18% -> 46% of each run, Pallas kernels for 0% -> 0%
where the time goes in v1:
time: 464 us; the launch traced here: 456 us
  waiting for transfers between devices  122 us (26%)
  local copies, waits for them, and re-layouts  97 us (21%)
  starting transfers between devices  93.2 us (20%)
  matrix products  87.1 us (19%)
  other arithmetic  53.8 us (12%)
    ppermute x45, waiting for transfers between devices, send(): return lax.ppermute(value, 'dp', pairs)  86.2 us
    ppermute x45, starting transfers between devices, send(): return lax.ppermute(value, 'dp', pairs)  67.7 us
    dynamic_update_slice x21, local copies, waits for them, and re-layouts, put(): lax.dynamic_update_slice(buffer, jnp.expand_dims(piece, axis), tuple(star...  46.2 us
    dot_general x18, matrix products, dot(): return lax.dot_general(a, b, (dims, ((), ())), preferred_element_type=F32)  43.9 us
    ppermute x13, waiting for transfers between devices, half_swap(): return lax.ppermute(value, 'mp', HALF_SWAP)  36.2 us
    unnamed x175, local copies, waits for them, and re-layouts  17.7 us
    ppermute x13, starting transfers between devices, half_swap(): return lax.ppermute(value, 'mp', HALF_SWAP)  14.1 us
    convert_element_type x1, other arithmetic, attend_back(): low = (probs * (d_probs - mean)).astype(BF16)  12.3 us
  transfers between devices with their start and end apart: 71, of which 15 were waited for; matrix products, arithmetic and copies ran while one was open for 46% of the time, Pallas kernels for 0%

profile of v1, /device:TPU:0, one launch (start us, length us, event | category | flops | bytes accessed | tf_op | source)
XLA Modules:
  0.0 456.2 jit_solution(4574845771732764254)
XLA Ops:
  4.0 5.1 %collective-permute-start.10 = (bf16[1,96,192]{2,1,0:T(8,128)(2,1)S(1)}, bf16[1,96,192]{2,1,0:T(8,128)(2,1)S(1)}, u32[]{:S(2)}, u32[]{:S(2)}) collective-permute-start(bf16[1,96,192]{2,1,0:T(8,128)(2,1)S(1)} %bitcast.291), channel_id=1, source_target_pairs={{0,24},{4,28},{8,0},{12,4},{16,8},{20,12},{24,16},{28,20},{1,25},{... | collective-permute-start | bytes 110600 | tf_op jit(solution)/shard_map/ppermute | solution.py:66
  25.9 3.8 collective-permute-start.23
  30.6 6.7 %collective-permute-start.21 = (bf16[1,96,768]{2,1,0:T(8,128)(2,1)}, bf16[1,96,768]{2,1,0:T(8,128)(2,1)}, u32[]{:S(2)}, u32[]{:S(2)}) collective-permute-start(bf16[1,96,768]{2,1,0:T(8,128)(2,1)} %convert_bitcast_fusion.1), channel_id=1, source_target_pairs={{0,8},{4,12},{8,16},{12,20},{16,24},{20,28},{24,0},{28,4},{1,9},{5... | collective-permute-start | bytes 442376 | tf_op jit(solution)/shard_map/ppermute | solution.py:66
  37.4 9.4 %collective-permute-done.3 = bf16[1,96,576]{1,2,0:T(8,128)(2,1)S(1)} collective-permute-done((bf16[1,96,576]{1,2,0:T(8,128)(2,1)S(1)}, bf16[1,96,576]{1,2,0:T(8,128)(2,1)S(1)}, u32[]{:S(2)}, u32[]{:S(2)}) %collective-permute-start.3) | collective-permute-done | bytes 110624 | tf_op jit(solution)/shard_map/ppermute | solution.py:66
  49.7 4.7 %collective-permute-done.15 = bf16[1,96,768]{2,1,0:T(8,128)(2,1)} collective-permute-done((bf16[1,96,768]{2,1,0:T(8,128)(2,1)S(1)}, bf16[1,96,768]{2,1,0:T(8,128)(2,1)}, u32[]{:S(2)}, u32[]{:S(2)}) %collective-permute-start.15) | collective-permute-done | bytes 147488 | tf_op jit(solution)/shard_map/ppermute | solution.py:66
  69.4 8.0 %collective-permute-done.5 = bf16[1,4,96,576]{3,2,1,0:T(8,128)(2,1)S(1)} collective-permute-done((bf16[1,4,96,576]{3,2,1,0:T(8,128)(2,1)S(1)}, bf16[1,4,96,576]{3,2,1,0:T(8,128)(2,1)S(1)}, u32[]{:S(2)}, u32[]{:S(2)}) %collective-permute-start.5) | collective-permute-done | bytes 442400 | tf_op jit(solution)/shard_map/ppermute | solution.py:66
  84.8 18.5 %dynamic_update_slice.92 = bf16[2,4,2,96,192]{3,2,1,4,0:T(2,128)(2,1)} dynamic-update-slice(bf16[2,4,2,96,192]{3,2,1,4,0:T(2,128)(2,1)} %broadcast_in_dim.183, bf16[2,4,1,96,192]{3,2,1,4,0:T(2,128)(2,1)S(1)} %copy.109, s32[]{:T(128)} %constant.191.clone.1, s32[]{:T(128)} %constant.191.clone.1, s32[]{:T(128)S(6)} %select_n.201, s32[]{:T(128)} %constant.191.clone.1, s32[]{:T(128)} %constant.191.clone.1) | dynamic-update-slice | bytes 589828 | tf_op jit(solution)/shard_map/dynamic_update_slice | solution.py:72
  105.8 18.5 %dynamic_update_slice.93 = bf16[2,4,2,96,192]{3,2,1,4,0:T(2,128)(2,1)} dynamic-update-slice(bf16[2,4,2,96,192]{3,2,1,4,0:T(2,128)(2,1)} %dynamic_update_slice.92, bf16[2,4,1,96,192]{3,2,1,4,0:T(2,128)(2,1)S(1)} %copy.110, s32[]{:T(128)} %constant.191.clone.1, s32[]{:T(128)} %constant.191.clone.1, s32[]{:T(128)S(6)} %select_n.202, s32[]{:T(128)} %constant.191.clone.1, s32[]{:T(128)} %constant.191.clone.1) | dynamic-update-slice | bytes 589828 | tf_op jit(solution)/shard_map/dynamic_update_slice | solution.py:72
  134.0 8.4 %fusion.130 = (f32[6,832]{1,0:T(8,128)S(1)}, f32[6,832,832]{1,2,0:T(8,128)}) fusion(bf16[832,3,3,64]{0,3,2,1:T(8,128)(2,1)S(1)} %bitcast.241, bf16[832,3,3,64]{0,3,2,1:T(8,128)(2,1)S(1)} %bitcast.236, pred[832,832]{0,1:T(8,128)(4,1)S(1)} %copy-done.15), kind=kOutput, calls=%fused_computation.299 | convolution fusion | flops 544722048 | bytes 21507584 | tf_op jit(solution)/shard_map/qhd,khd->hqk/dot_general | solution.py:205
  142.4 8.5 %fusion = f32[6,832]{1,0:T(8,128)S(1)} fusion(f32[6,832,832]{1,2,0:T(8,128)} %get-tuple-element.181, f32[6,832]{1,0:T(8,128)S(1)} %get-tuple-element.180), kind=kLoop, calls=%fused_computation.6 | loop fusion | flops 8301696 | bytes 16653312 | tf_op jit(solution)/shard_map/reduce_sum | solution.py:209
  151.0 9.4 %fusion.20 = bf16[6,64,832]{2,1,0:T(8,128)(2,1)S(1)} fusion(f32[6,832,832]{1,2,0:T(8,128)} %get-tuple-element.181, f32[6,832]{1,0:T(8,128)S(1)} %fusion, f32[6,832]{1,0:T(8,128)S(1)} %get-tuple-element.180, bf16[832,3,3,64]{0,3,2,1:T(8,128)(2,1)S(1)} %bitcast.237, bf16[832,3,3,64]{0,3,2,1:T(8,128)(2,1)S(1)} %bitcast.242), kind=kOutput, calls=%fused_computation.50 | convolution fusion | flops 544727040 | bytes 19209216 | tf_op jit(solution)/shard_map/hqk,khd->qhd/dot_general | solution.py:211
  170.1 24.6 %collective-permute-done.25 = bf16[2,4,96,768]{3,2,1,0:T(8,128)(2,1)S(1)} collective-permute-done((bf16[2,4,96,768]{3,2,1,0:T(8,128)(2,1)S(1)}, bf16[2,4,96,768]{3,2,1,0:T(8,128)(2,1)S(1)}, u32[]{:S(2)}, u32[]{:S(2)}) %collective-permute-start.25) | collective-permute-done | bytes 1179680 | tf_op jit(solution)/shard_map/ppermute | solution.py:66
  195.1 4.4 multiply_convert_fusion.2
  221.7 6.1 %convert_reduce_fusion = (f32[1536]{0:T(1024)S(1)}, bf16[832,1536]{1,0:T(8,128)(2,1)S(1)}) fusion(f32[832,1536]{1,0:T(8,128)} %get-tuple-element.183, f32[1536]{0:T(1024)S(1)} %copy-done.64, bf16[768,768]{1,0:T(8,128)(2,1)S(1)} %bitcast.281, bf16[768,768]{1,0:T(8,128)(2,1)S(1)} %bitcast.279, bf16[416,768]{1,0:T(8,128)(2,1)S(1)} %collective-permute-done.29, ...), kind=kOutput, calls=%fused_computation.17 | convolution fusion | flops 1989376512 | bytes 11317248 | tf_op jit(solution)/shard_map/dot_general | solution.py:23
  230.2 4.8 %collective-permute-start.30 = (bf16[416,768]{1,0:T(8,128)(2,1)S(1)}, bf16[416,768]{1,0:T(8,128)(2,1)S(1)}, u32[]{:S(2)}, u32[]{:S(2)}) collective-permute-start(bf16[416,768]{1,0:T(8,128)(2,1)S(1)} %slice.305), channel_id=1, source_target_pairs={{0,1},{1,0},{2,3},{3,2},{4,5},{5,4},{6,7},{7,6},{8,9},{9,8},{10,11... | collective-permute-start | bytes 1916936 | tf_op jit(solution)/shard_map/ppermute | solution.py:31
  258.7 7.3 %collective-permute-done.45 = bf16[4,96,768]{2,1,0:T(8,128)(2,1)} collective-permute-done((bf16[4,96,768]{2,1,0:T(8,128)(2,1)}, bf16[4,96,768]{2,1,0:T(8,128)(2,1)}, u32[]{:S(2)}, u32[]{:S(2)}) %collective-permute-start.45) | collective-permute-done | bytes 589856 | tf_op jit(solution)/shard_map/ppermute | solution.py:66
  272.7 20.5 %collective-permute-done.69 = f32[6,768]{1,0:T(8,128)S(1)} collective-permute-done((f32[6,768]{1,0:T(8,128)S(1)}, f32[6,768]{1,0:T(8,128)S(1)}, u32[]{:S(2)}, u32[]{:S(2)}) %collective-permute-start.69) | collective-permute-done | bytes 18464 | tf_op jit(solution)/shard_map/ppermute | solution.py:35
  308.4 9.2 %fusion.34 = bf16[832,6,64]{0,2,1:T(8,128)(2,1)S(1)} fusion(bf16[832,6,64]{0,2,1:T(8,128)(2,1)} %bitcast.247, f32[6,832,832]{1,2,0:T(8,128)} %get-tuple-element.181, f32[6,832]{1,0:T(8,128)S(1)} %log_add_fusion), kind=kOutput, calls=%fused_computation.88 | convolution fusion | flops 540254208 | bytes 17911296 | tf_op jit(solution)/shard_map/hqk,qhd->khd/dot_general | solution.py:220
  317.6 11.7 %multiply_reduce_fusion = (f32[6,832]{1,0:T(8,128)S(1)}, f32[6,832,832]{1,2,0:T(8,128)}) fusion(f32[6,832,832]{1,2,0:T(8,128)} %get-tuple-element.181, f32[6,832]{1,0:T(8,128)S(1)} %log_add_fusion, bf16[832,6,64]{0,2,1:T(8,128)(2,1)S(1)} %bitcast.248, bf16[832,3,3,64]{0,3,2,1:T(8,128)(2,1)S(1)} %bitcast.238, bf16[832,3,3,64]{0,3,2,1:T(8,128)(2,1)S(1)} %bitcast.243), kind=kOutput, calls=%fused_computation.1 | convolution fusion | flops 544402560 | bytes 35822592 | tf_op jit(solution)/shard_map/qhd,khd->hqk/dot_general | solution.py:221
  329.3 12.3 %multiply_convert_fusion = bf16[6,832,832]{1,2,0:T(8,128)(2,1)S(1)} fusion(f32[6,832,832]{1,2,0:T(8,128)} %get-tuple-element.185, f32[6,832,832]{1,2,0:T(8,128)} %get-tuple-element.181, f32[6,832]{1,0:T(8,128)S(1)} %get-tuple-element.184, f32[6,832]{1,0:T(8,128)S(1)} %log_add_fusion), kind=kLoop, calls=%fused_computation | loop fusion | flops 16613376 | bytes 41573376 | tf_op jit(solution)/shard_map/convert_element_type | solution.py:223
  383.1 13.2 %collective-permute-done.40 = bf16[4,96,192]{1,2,0:T(8,128)(2,1)S(1)} collective-permute-done((bf16[4,96,192]{1,2,0:T(8,128)(2,1)S(1)}, bf16[4,96,192]{1,2,0:T(8,128)(2,1)S(1)}, u32[]{:S(2)}, u32[]{:S(2)}) %collective-permute-start.40) | collective-permute-done | bytes 147488 | tf_op jit(solution)/shard_map/ppermute | solution.py:66
  410.7 15.7 %collective-permute-done.34 = bf16[4,2,96,576]{3,2,1,0:T(8,128)(2,1)S(1)} collective-permute-done((bf16[4,2,96,576]{3,2,1,0:T(8,128)(2,1)S(1)}, bf16[4,2,96,576]{3,2,1,0:T(8,128)(2,1)S(1)}, u32[]{:S(2)}, u32[]{:S(2)}) %collective-permute-start.34) | collective-permute-done | bytes 884768 | tf_op jit(solution)/shard_map/ppermute | solution.py:35
  430.1 8.7 %collective-permute-done.35 = bf16[4,96,576]{2,1,0:T(8,128)(2,1)S(1)} collective-permute-done((bf16[4,96,576]{2,1,0:T(8,128)(2,1)S(1)}, bf16[4,96,576]{2,1,0:T(8,128)(2,1)S(1)}, u32[]{:S(2)}, u32[]{:S(2)}) %collective-permute-start.35) | collective-permute-done | bytes 442400 | tf_op jit(solution)/shard_map/ppermute | solution.py:66
  446.9 5.2 %collective-permute-done.37 = bf16[96,576]{1,0:T(8,128)(2,1)S(1)} collective-permute-done((bf16[96,576]{1,0:T(8,128)(2,1)S(1)}, bf16[96,576]{1,0:T(8,128)(2,1)S(1)}, u32[]{:S(2)}, u32[]{:S(2)}) %collective-permute-start.37) | collective-permute-done | bytes 110624 | tf_op jit(solution)/shard_map/ppermute | solution.py:66
  (471 shorter events, 208.7 us)
Async XLA Ops:
  4.0 25.8 %collective-permute-start.10 = (bf16[1,96,192]{2,1,0:T(8,128)(2,1)S(1)}, bf16[1,96,192]{2,1,0:T(8,128)(2,1)S(1)}, u32[]{:S(2)}, u32[]{:S(2)}) collective-permute-start(bf16[1,96,192]{2,1,0:T(8,128)(2,1)S(1)} %bitcast.291), channel_id=1, source_target_pairs={{0,24},{4,28},{8,0},{12,4},{16,8},{20,12},{24,16},{28,20},{1,25},{... | collective-permute-start | bytes 110600 | tf_op jit(solution)/shard_map/ppermute | solution.py:66
  25.9 37.3 %collective-permute-start.23 = (bf16[1,96,768]{2,1,0:T(8,128)(2,1)}, bf16[1,96,768]{2,1,0:T(8,128)(2,1)}, u32[]{:S(2)}, u32[]{:S(2)}) collective-permute-start(bf16[1,96,768]{2,1,0:T(8,128)(2,1)} %convert_bitcast_fusion.1), channel_id=1, source_target_pairs={{0,24},{4,28},{8,0},{12,4},{16,8},{20,12},{24,16},{28,20},{1,25},{... | collective-permute-start | bytes 442376 | tf_op jit(solution)/shard_map/ppermute | solution.py:66
  30.5 31.7 %collective-permute-start.22 = (bf16[1,96,768]{2,1,0:T(8,128)(2,1)}, bf16[1,96,768]{2,1,0:T(8,128)(2,1)}, u32[]{:S(2)}, u32[]{:S(2)}) collective-permute-start(bf16[1,96,768]{2,1,0:T(8,128)(2,1)} %convert_bitcast_fusion.1), channel_id=1, source_target_pairs={{0,16},{4,20},{8,24},{12,28},{16,0},{20,4},{24,8},{28,12},{1,17},{... | collective-permute-start | bytes 442376 | tf_op jit(solution)/shard_map/ppermute | solution.py:66
  30.6 29.1 %collective-permute-start.21 = (bf16[1,96,768]{2,1,0:T(8,128)(2,1)}, bf16[1,96,768]{2,1,0:T(8,128)(2,1)}, u32[]{:S(2)}, u32[]{:S(2)}) collective-permute-start(bf16[1,96,768]{2,1,0:T(8,128)(2,1)} %convert_bitcast_fusion.1), channel_id=1, source_target_pairs={{0,8},{4,12},{8,16},{12,20},{16,24},{20,28},{24,0},{28,4},{1,9},{5... | collective-permute-start | bytes 442376 | tf_op jit(solution)/shard_map/ppermute | solution.py:66
  46.8 31.2 %collective-permute-start.17 = (bf16[1,96,768]{2,1,0:T(8,128)(2,1)S(1)}, bf16[1,96,768]{2,1,0:T(8,128)(2,1)}, u32[]{:S(2)}, u32[]{:S(2)}) collective-permute-start(bf16[1,96,768]{2,1,0:T(8,128)(2,1)S(1)} %convert_bitcast_fusion.2), channel_id=1, source_target_pairs={{0,24},{4,28},{8,0},{12,4},{16,8},{20,12},{24,16},{28,20},{1,25},{... | collective-permute-start | bytes 442376 | tf_op jit(solution)/shard_map/ppermute | solution.py:66
  62.2 66.1 %collective-permute-start.1 = (bf16[416,768]{1,0:T(8,128)(2,1)S(1)}, bf16[416,768]{1,0:T(8,128)(2,1)}, u32[]{:S(2)}, u32[]{:S(2)}) collective-permute-start(bf16[416,768]{1,0:T(8,128)(2,1)S(1)} %select_dynamic-update-slice_fusion.3), channel_id=1, source_target_pairs={{0,1},{1,0},{2,3},{3,2},{4,5},{5,4},{6,7},{7,6},{8,9},{9,8},{10,11... | collective-permute-start | bytes 1916936 | tf_op jit(solution)/shard_map/ppermute | solution.py:31
  65.7 99.7 %collective-permute-start.24 = (bf16[1,4,96,768]{3,2,1,0:T(8,128)(2,1)S(1)}, bf16[1,4,96,768]{3,2,1,0:T(8,128)(2,1)}, u32[]{:S(2)}, u32[]{:S(2)}) collective-permute-start(bf16[1,4,96,768]{3,2,1,0:T(8,128)(2,1)S(1)} %bitcast_dynamic-update-slice_fusion.7), channel_id=1, source_target_pairs={{0,2},{2,0},{1,3},{3,1},{4,6},{6,4},{5,7},{7,5},{8,10},{10,8},{9,1... | collective-permute-start | bytes 1769480 | tf_op jit(solution)/shard_map/ppermute | solution.py:35
  67.9 35.4 %collective-permute-start.12 = (bf16[2,4,96,192]{3,2,1,0:T(8,128)(2,1)}, bf16[2,4,96,192]{3,2,1,0:T(8,128)(2,1)}, u32[]{:S(2)}, u32[]{:S(2)}) collective-permute-start(bf16[2,4,96,192]{3,2,1,0:T(8,128)(2,1)} %get-tuple-element.167), channel_id=1, source_target_pairs={{0,4},{4,0},{8,12},{12,8},{16,20},{20,16},{24,28},{28,24},{1,5},{5... | collective-permute-start | bytes 884744 | tf_op jit(solution)/shard_map/ppermute | solution.py:66
  77.5 53.9 %collective-permute-start.6 = (bf16[1,4,2,96,576]{4,3,2,1,0:T(8,128)(2,1)S(1)}, bf16[1,4,2,96,576]{4,3,2,1,0:T(8,128)(2,1)}, u32[]{:S(2)}, u32[]{:S(2)}) collective-permute-start(bf16[1,4,2,96,576]{4,3,2,1,0:T(8,128)(2,1)S(1)} %bitcast_dynamic-update-slice_fusion.5), channel_id=1, source_target_pairs={{0,2},{2,0},{1,3},{3,1},{4,6},{6,4},{5,7},{7,5},{8,10},{10,8},{9,1... | collective-permute-start | bytes 2654216 | tf_op jit(solution)/shard_map/ppermute | solution.py:35
  79.6 83.0 %collective-permute-start.18 = (bf16[1,4,96,768]{3,2,1,0:T(8,128)(2,1)}, bf16[1,4,96,768]{3,2,1,0:T(8,128)(2,1)}, u32[]{:S(2)}, u32[]{:S(2)}) collective-permute-start(bf16[1,4,96,768]{3,2,1,0:T(8,128)(2,1)} %bitcast_dynamic-update-slice_fusion.10), channel_id=1, source_target_pairs={{0,4},{4,0},{8,12},{12,8},{16,20},{20,16},{24,28},{28,24},{1,5},{5... | collective-permute-start | bytes 1769480 | tf_op jit(solution)/shard_map/ppermute | solution.py:66
  163.8 31.2 %collective-permute-start.19 = (bf16[1,4,2,96,768]{4,3,2,1,0:T(8,128)(2,1)S(1)}, bf16[1,4,2,96,768]{4,3,2,1,0:T(8,128)(2,1)S(1)}, u32[]{:S(2)}, u32[]{:S(2)}) collective-permute-start(bf16[1,4,2,96,768]{4,3,2,1,0:T(8,128)(2,1)S(1)} %bitcast_dynamic-update-slice_fusion.3), channel_id=1, source_target_pairs={{0,2},{2,0},{1,3},{3,1},{4,6},{6,4},{5,7},{7,5},{8,10},{10,8},{9,1... | collective-permute-start | bytes 3538952 | tf_op jit(solution)/shard_map/ppermute | solution.py:35
  166.6 28.2 %collective-permute-start.25 = (bf16[2,4,96,768]{3,2,1,0:T(8,128)(2,1)S(1)}, bf16[2,4,96,768]{3,2,1,0:T(8,128)(2,1)S(1)}, u32[]{:S(2)}, u32[]{:S(2)}) collective-permute-start(bf16[2,4,96,768]{3,2,1,0:T(8,128)(2,1)S(1)} %pad_maximum_fusion.10), channel_id=1, source_target_pairs={{0,4},{4,0},{8,12},{12,8},{16,20},{20,16},{24,28},{28,24},{1,5},{5... | collective-permute-start | bytes 3538952 | tf_op jit(solution)/shard_map/ppermute | solution.py:66
  168.2 26.9 %collective-permute-start.14 = (bf16[416,768]{1,0:T(8,128)(2,1)S(1)}, bf16[416,768]{1,0:T(8,128)(2,1)S(1)}, u32[]{:S(2)}, u32[]{:S(2)}) collective-permute-start(bf16[416,768]{1,0:T(8,128)(2,1)S(1)} %fusion.42), channel_id=1, source_target_pairs={{0,1},{1,0},{2,3},{3,2},{4,5},{5,4},{6,7},{7,6},{8,9},{9,8},{10,11... | collective-permute-start | bytes 1916936 | tf_op jit(solution)/shard_map/ppermute | solution.py:31
  237.4 57.8 %collective-permute-start.44 = (bf16[4,96,768]{2,1,0:T(8,128)(2,1)}, bf16[4,96,768]{2,1,0:T(8,128)(2,1)}, u32[]{:S(2)}, u32[]{:S(2)}) collective-permute-start(bf16[4,96,768]{2,1,0:T(8,128)(2,1)} %dynamic-slice_bitcast_fusion.1), channel_id=1, source_target_pairs={{0,4},{4,0},{8,12},{12,8},{16,20},{20,16},{24,28},{28,24},{1,5},{5... | collective-permute-start | bytes 1769480 | tf_op jit(solution)/shard_map/ppermute | solution.py:66
  240.4 25.5 %collective-permute-start.45 = (bf16[4,96,768]{2,1,0:T(8,128)(2,1)}, bf16[4,96,768]{2,1,0:T(8,128)(2,1)}, u32[]{:S(2)}, u32[]{:S(2)}) collective-permute-start(bf16[4,96,768]{2,1,0:T(8,128)(2,1)} %dynamic-slice_bitcast_fusion), channel_id=1, source_target_pairs={{0,4},{4,0},{8,12},{12,8},{16,20},{20,16},{24,28},{28,24},{1,5},{5... | collective-permute-start | bytes 1769480 | tf_op jit(solution)/shard_map/ppermute | solution.py:66
  254.1 47.1 %collective-permute-start.50 = (bf16[4,2,96,768]{3,2,0,1:T(8,128)(2,1)}, bf16[4,2,96,768]{3,2,0,1:T(8,128)(2,1)S(1)}, u32[]{:S(2)}, u32[]{:S(2)}) collective-permute-start(bf16[4,2,96,768]{3,2,0,1:T(8,128)(2,1)} %copy.125), channel_id=1, source_target_pairs={{0,2},{2,0},{1,3},{3,1},{4,6},{6,4},{5,7},{7,5},{8,10},{10,8},{9,1... | collective-permute-start | bytes 3538952 | tf_op jit(solution)/shard_map/ppermute | solution.py:35
  256.2 37.0 %collective-permute-start.64 = (f32[768]{0:T(1024)S(1)}, f32[768]{0:T(1024)S(1)}, u32[]{:S(2)}, u32[]{:S(2)}) collective-permute-start(f32[768]{0:T(1024)S(1)} %add_add_fusion.1), channel_id=1, source_target_pairs={{0,4},{4,0},{8,12},{12,8},{16,20},{20,16},{24,28},{28,24},{1,5},{5... | collective-permute-start | bytes 9224 | tf_op jit(solution)/shard_map/ppermute | solution.py:66
  267.3 27.9 %collective-permute-start.46 = (bf16[4,96,768]{2,1,0:T(8,128)(2,1)S(1)}, bf16[4,96,768]{2,1,0:T(8,128)(2,1)S(1)}, u32[]{:S(2)}, u32[]{:S(2)}) collective-permute-start(bf16[4,96,768]{2,1,0:T(8,128)(2,1)S(1)} %fusion.40), channel_id=1, source_target_pairs={{0,2},{2,0},{1,3},{3,1},{4,6},{6,4},{5,7},{7,5},{8,10},{10,8},{9,1... | collective-permute-start | bytes 1769480 | tf_op jit(solution)/shard_map/ppermute | solution.py:35
  269.2 24.1 %collective-permute-start.69 = (f32[6,768]{1,0:T(8,128)S(1)}, f32[6,768]{1,0:T(8,128)S(1)}, u32[]{:S(2)}, u32[]{:S(2)}) collective-permute-start(f32[6,768]{1,0:T(8,128)S(1)} %add.535), channel_id=1, source_target_pairs={{0,2},{2,0},{1,3},{3,1},{4,6},{6,4},{5,7},{7,5},{8,10},{10,8},{9,1... | collective-permute-start | bytes 55304 | tf_op jit(solution)/shard_map/ppermute | solution.py:35
  297.3 99.1 %collective-permute-start.47 = (bf16[96,768]{1,0:T(8,128)(2,1)}, bf16[96,768]{1,0:T(8,128)(2,1)S(1)}, u32[]{:S(2)}, u32[]{:S(2)}) collective-permute-start(bf16[96,768]{1,0:T(8,128)(2,1)} %get-tuple-element.147), channel_id=1, source_target_pairs={{0,8},{4,12},{8,16},{12,20},{16,24},{20,28},{24,0},{28,4},{1,9},{5... | collective-permute-start | bytes 442376 | tf_op jit(solution)/shard_map/ppermute | solution.py:66
  298.5 98.8 %collective-permute-start.49 = (bf16[96,768]{1,0:T(8,128)(2,1)}, bf16[96,768]{1,0:T(8,128)(2,1)}, u32[]{:S(2)}, u32[]{:S(2)}) collective-permute-start(bf16[96,768]{1,0:T(8,128)(2,1)} %get-tuple-element.148), channel_id=1, source_target_pairs={{0,24},{4,28},{8,0},{12,4},{16,8},{20,12},{24,16},{28,20},{1,25},{... | collective-permute-start | bytes 442376 | tf_op jit(solution)/shard_map/ppermute | solution.py:66
  364.0 36.3 %collective-permute-start.48 = (bf16[96,768]{1,0:T(8,128)(2,1)}, bf16[96,768]{1,0:T(8,128)(2,1)}, u32[]{:S(2)}, u32[]{:S(2)}) collective-permute-start(bf16[96,768]{1,0:T(8,128)(2,1)} %get-tuple-element.149), channel_id=1, source_target_pairs={{0,16},{4,20},{8,24},{12,28},{16,0},{20,4},{24,8},{28,12},{1,17},{... | collective-permute-start | bytes 442376 | tf_op jit(solution)/shard_map/ppermute | solution.py:66
  379.0 27.3 %collective-permute-start.51 = (bf16[4,96,768]{2,1,0:T(8,128)(2,1)}, bf16[4,96,768]{2,1,0:T(8,128)(2,1)S(1)}, u32[]{:S(2)}, u32[]{:S(2)}) collective-permute-start(bf16[4,96,768]{2,1,0:T(8,128)(2,1)} %fusion.48), channel_id=1, source_target_pairs={{0,4},{4,0},{8,12},{12,8},{16,20},{20,16},{24,28},{28,24},{1,5},{5... | collective-permute-start | bytes 1769480 | tf_op jit(solution)/shard_map/ppermute | solution.py:66
  402.9 23.5 %collective-permute-start.34 = (bf16[4,2,96,576]{3,2,1,0:T(8,128)(2,1)S(1)}, bf16[4,2,96,576]{3,2,1,0:T(8,128)(2,1)S(1)}, u32[]{:S(2)}, u32[]{:S(2)}) collective-permute-start(bf16[4,2,96,576]{3,2,1,0:T(8,128)(2,1)S(1)} %bitcast.283), channel_id=1, source_target_pairs={{0,2},{2,0},{1,3},{3,1},{4,6},{6,4},{5,7},{7,5},{8,10},{10,8},{9,1... | collective-permute-start | bytes 2654216 | tf_op jit(solution)/shard_map/ppermute | solution.py:35
  (128 other events, 1608.3 us)

commit v2 on v1

--- a/solution.py
+++ b/solution.py
@@ -3,6 +3,8 @@
 import jax
 import jax.numpy as jnp
 from jax import lax
+from jax.experimental import pallas as pl
+from jax.experimental.pallas import tpu as pltpu
 from jax.sharding import PartitionSpec as P
 
 HEAD_DIM = 64
@@ -128,6 +130,16 @@
     return value
 
 
+def sum_half(grid, pair):
+    value = pair[0] + half_swap(pair[1])
+    for stage in range(len(grid.dims)):
+        total = value
+        for ahead in range(1, grid.dims[stage]):
+            total = total + grid.send(value, stage, ahead)
+        value = total
+    return value
+
+
 def sum_all(grid, value, over_cores):
     for stage in range(len(grid.dims)):
         total = value
@@ -176,12 +188,408 @@
     return jnp.where(member == 3, placed, rows)
 
 
-def send_back(rows, member):
+def put_back(rows, moved, member):
     source, free, count = move_plan(rows.shape[0])
-    moved = lax.ppermute(rows[free : free + count], "mp", [(3, 1)])
     placed = lax.dynamic_update_slice(rows, moved, (source, 0))
     cleared = lax.dynamic_update_slice(rows, jnp.zeros_like(moved), (free, 0))
     return jnp.where(member == 1, placed, jnp.where(member == 3, cleared, rows))
+
+
+def send_back(rows, member):
+    source, free, count = move_plan(rows.shape[0])
+    return put_back(rows, lax.ppermute(rows[free : free + count], "mp", [(3, 1)]), member)
+
+
+CHAIN = 4
+X_FIRST = (False, True, True, False)
+WHERE = [(0, 0)] + [(step, sign) for step in range(1, CHAIN) for sign in (1, -1)]
+
+
+class Place:
+    def __init__(self):
+        self.dp = lax.axis_index("dp")
+        self.mp = lax.axis_index("mp")
+        self.z = self.dp // 2
+        self.x = lax.rem(self.dp, 2)
+        self.up = (self.dp + 2, self.mp)
+        self.down = (self.dp - 2, self.mp)
+        self.across = (self.dp + 1 - 2 * self.x, self.mp)
+        self.other = (self.dp, lax.rem(self.mp + 2, 4))
+        self.mate = (self.dp, self.mp + 1 - 2 * lax.rem(self.mp, 2))
+        self.has_up = self.z < CHAIN - 1
+        self.has_down = self.z > 0
+
+    def ring(self, ahead):
+        return (lax.rem(self.dp + 2 * ahead, 2 * CHAIN), self.mp)
+
+    def greet(self, peers):
+        barrier = pltpu.get_barrier_semaphore()
+        for peer in peers:
+            pl.semaphore_signal(
+                barrier, inc=1, device_id=peer, device_id_type=pl.DeviceIdType.MESH
+            )
+        pl.semaphore_wait(barrier, len(peers))
+
+
+def remote(source, target, sends, arrivals, index, device):
+    return pltpu.make_async_remote_copy(
+        source,
+        target,
+        sends.at[index],
+        arrivals.at[index],
+        device_id=device,
+        device_id_type=pl.DeviceIdType.MESH,
+    )
+
+
+def gather_kernel(row_plan, *refs):
+    shards, (rows_ref, cot_ref, vec_ref) = refs[0:4], refs[4:7]
+    fulls, (rows_out, cot_out, vec_out) = refs[7:11], refs[11:14]
+    sends, arrivals, side_send, side_arrive, local = refs[14:19]
+    here = Place()
+    source, free, count = row_plan
+    n_rows = rows_ref.shape[0]
+    here.greet([here.ring(1), here.ring(2), here.ring(3), here.across, here.other, here.mate,
+                (here.dp, 3 - here.mp)])
+
+    def z_of(where):
+        step, sign = where
+        return here.z - step * sign
+
+    def held(where):
+        step, sign = where
+        if step == 0:
+            return None
+        return here.z >= step if sign > 0 else here.z + step < CHAIN
+
+    def maybe(condition, action):
+        if condition is None:
+            action()
+        else:
+            pl.when(condition)(action)
+
+    def block(w, where, far, half):
+        x = 1 - here.x if far else here.x
+        return fulls[w].at[half, z_of(where) * 2 + x]
+
+    def chain(w, where):
+        step, sign = where
+        origin = shards[w] if step == 0 else block(w, where, False, 0)
+        jobs = []
+        for way in (1, -1) if step == 0 else (sign,):
+            index = step + (0 if way > 0 else 3)
+            device = here.up if way > 0 else here.down
+            go = here.has_up if way > 0 else here.has_down
+            if step < CHAIN - 1:
+                jobs.append((go, remote(origin, block_to(w, where), sends.at[w], arrivals.at[w], index, device)))
+        return jobs
+
+    def block_to(w, where):
+        return fulls[w].at[0, z_of(where) * 2 + here.x]
+
+    def second(w, where):
+        origin = shards[w] if where[0] == 0 else block(w, where, False, 0)
+        index = 6 + WHERE.index(where)
+        if X_FIRST[w]:
+            return remote(origin, block(w, where, False, 0), sends.at[w], arrivals.at[w], index, here.across)
+        return remote(origin, block(w, where, False, 1), sends.at[w], arrivals.at[w], index, here.other)
+
+    def third(w, where, arrived):
+        index = 13 + WHERE.index(where) + (len(WHERE) if arrived else 0)
+        if X_FIRST[w]:
+            origin = shards[w] if where[0] == 0 and not arrived else block(w, where, arrived, 0)
+            return remote(origin, block(w, where, arrived, 1), sends.at[w], arrivals.at[w], index, here.other)
+        origin = shards[w] if where[0] == 0 and not arrived else block(w, where, False, int(arrived))
+        return remote(origin, block(w, where, False, int(arrived)), sends.at[w], arrivals.at[w], index, here.across)
+
+    def landing(w, where, stage, arrived=False):
+        if stage == 2:
+            index = 6 + WHERE.index(where)
+            target = block(w, where, True, 0) if X_FIRST[w] else block(w, where, False, 1)
+            device = here.across if X_FIRST[w] else here.other
+        else:
+            index = 13 + WHERE.index(where) + (len(WHERE) if arrived else 0)
+            if X_FIRST[w]:
+                target, device = block(w, where, arrived, 1), here.other
+            else:
+                target, device = block(w, where, True, int(arrived)), here.across
+        return remote(target, target, sends.at[w], arrivals.at[w], index, device)
+
+    def chain_landing(w, where):
+        step, sign = where
+        index = step - 1 + (0 if sign > 0 else 3)
+        target = block(w, where, False, 0)
+        return remote(target, target, sends.at[w], arrivals.at[w], index, here.down if sign > 0 else here.up)
+
+    order = (0, 1, 3, 2)
+    by_step = [[p for p in WHERE if p[0] == step] for step in range(CHAIN)]
+
+    low, high = pl.ds(0, free), pl.ds(free + count, n_rows - free - count)
+    middle, tail = pl.ds(free, count), pl.ds(source, count)
+    locals_ = [(None, pltpu.make_async_copy(shards[w], fulls[w].at[0, here.dp], local.at[w])) for w in order]
+    not_last, second_core = here.mp != 3, here.mp == 1
+    for n, (given, taken) in enumerate(((rows_ref, rows_out.at[0]), (cot_ref, cot_out))):
+        for m, part in enumerate((low, high, middle)):
+            copy = pltpu.make_async_copy(given.at[part], taken.at[part], local.at[4 + 3 * n + m])
+            locals_.append((not_last if m == 2 else None, copy))
+    for condition, copy in locals_:
+        maybe(condition, copy.start)
+
+    def to_mate(m, part):
+        return remote(rows_ref.at[part], rows_out.at[1, part], side_send, side_arrive, m, here.mate)
+
+    side = [(None, to_mate(0, low)), (None, to_mate(1, high)), (not_last, to_mate(2, middle))]
+    side.append((None, remote(vec_ref, vec_out, side_send, side_arrive, 3, here.other)))
+    moved = [
+        remote(rows_ref.at[tail], rows_out.at[0, middle], side_send, side_arrive, 4, here.other),
+        remote(cot_ref.at[tail], cot_out.at[middle], side_send, side_arrive, 5, here.other),
+        remote(rows_ref.at[tail], rows_out.at[1, middle], side_send, side_arrive, 6, (here.dp, 3 - here.mp)),
+    ]
+    side += [(second_core, copy) for copy in moved]
+
+    started = []
+
+    def start(condition, copy):
+        maybe(condition, copy.start)
+        started.append((condition, copy))
+
+    for condition, copy in side:
+        start(condition, copy)
+    for step in range(CHAIN):
+        for where in by_step[step]:
+            for w in order:
+                if step > 0:
+                    maybe(held(where), chain_landing(w, where).wait_recv)
+                for go, copy in chain(w, where):
+                    both = go if held(where) is None else jnp.logical_and(go, held(where))
+                    start(both, copy)
+                start(held(where), second(w, where))
+                start(held(where), third(w, where, False))
+        for where in by_step[step - 1] if step > 0 else ():
+            for w in order:
+                maybe(held(where), landing(w, where, 2).wait_recv)
+                start(held(where), third(w, where, True))
+    for where in by_step[CHAIN - 1]:
+        for w in order:
+            maybe(held(where), landing(w, where, 2).wait_recv)
+            start(held(where), third(w, where, True))
+    for where in WHERE:
+        for w in order:
+            for arrived in (False, True):
+                maybe(held(where), landing(w, where, 3, arrived).wait_recv)
+    to_mate(0, low).wait_recv()
+    to_mate(1, high).wait_recv()
+    pl.when(here.mp != 2)(to_mate(2, middle).wait_recv)
+    side[3][1].wait_recv()
+    pl.when(here.mp == 3)(moved[0].wait_recv)
+    pl.when(here.mp == 3)(moved[1].wait_recv)
+    pl.when(here.mp == 2)(moved[2].wait_recv)
+    for condition, copy in started:
+        maybe(condition, copy.wait_send)
+    for condition, copy in locals_:
+        maybe(condition, copy.wait)
+
+
+def gather_all(shards, rows, cotangent, vectors):
+    rows_local, width = rows.shape
+    vmem, anywhere = pl.BlockSpec(memory_space=pltpu.VMEM), pl.BlockSpec(memory_space=pl.ANY)
+    shapes = [jax.ShapeDtypeStruct((2, 2 * CHAIN) + s.shape, s.dtype) for s in shards]
+    shapes += [
+        jax.ShapeDtypeStruct((2, rows_local, width), rows.dtype),
+        jax.ShapeDtypeStruct((rows_local, width), rows.dtype),
+        jax.ShapeDtypeStruct(vectors.shape, vectors.dtype),
+    ]
+    plan = move_plan(rows_local)
+    return pl.pallas_call(
+        lambda *refs: gather_kernel(plan, *refs),
+        out_shape=shapes,
+        in_specs=[vmem] * 7,
+        out_specs=[anywhere] * 6 + [vmem],
+        scratch_shapes=[
+            pltpu.SemaphoreType.DMA((4, 27)),
+            pltpu.SemaphoreType.DMA((4, 27)),
+            pltpu.SemaphoreType.DMA((7,)),
+            pltpu.SemaphoreType.DMA((7,)),
+            pltpu.SemaphoreType.DMA((10,)),
+        ],
+        compiler_params=pltpu.CompilerParams(
+            collective_id=0, has_side_effects=True, vmem_limit_bytes=16 * 2**20
+        ),
+        name="gather_all",
+    )(*shards, rows, cotangent, vectors)
+
+
+def scatter_kernel(*refs):
+    mine, theirs = refs[0:4], refs[4:8]
+    vec_ref, out_edge, grad_edge = refs[8:11]
+    sums, (vec_out, out_back, grad_back) = refs[11:15], refs[15:18]
+    firsts, seconds, rises, falls = refs[18:22], refs[22:26], refs[26:30], refs[30:34]
+    vec_in, sends, arrivals, side_send, side_arrive = refs[34:39]
+    here = Place()
+    here.greet([here.ring(1), here.ring(2), here.ring(3), here.across, here.other, here.mate])
+    order = (2, 3, 1, 0)
+    targets = (3, 0, 2, 1)
+    far = 1 - here.x
+    started = []
+
+    def start(copy, condition=None):
+        if condition is None:
+            copy.start()
+        else:
+            pl.when(condition)(copy.start)
+        started.append((condition, copy))
+        return copy
+
+    def add(target, more):
+        target[...] = (target[...].astype(F32) + more[...].astype(F32)).astype(BF16)
+
+    edges = []
+    for index, (given, taken) in enumerate(((out_edge, out_back), (grad_edge, grad_back))):
+        copy = remote(given, taken, side_send, side_arrive, 6 + index, here.other)
+        edges.append(start(copy, here.mp == 3))
+
+    def vec_send(index, device):
+        copy = remote(vec_out, vec_in.at[index], side_send, side_arrive, index, device)
+        copy.start()
+        return copy
+
+    vec_out[...] = vec_ref[...]
+    sent = vec_send(0, here.other)
+
+    first_jobs, second_jobs = {}, {}
+    for target in targets:
+        for w in order:
+            for part in (0, 1):
+                if X_FIRST[w]:
+                    origin, device = theirs[w].at[target, part], here.other
+                else:
+                    origin, device = (mine, theirs)[part][w].at[target, far], here.across
+                landed = firsts[w].at[target, part]
+                first_jobs[w, target, part] = start(
+                    remote(origin, landed, sends.at[w], arrivals.at[w], 2 * target + part, device)
+                )
+    sent.wait()
+    vec_out[0:6] = vec_out[0:6] + vec_in[0, 0:6]
+    vec_out[6:8] = vec_out[6:8] + vec_in[0, 8:10]
+    sent = vec_send(1, here.across)
+
+    for target in targets:
+        for w in order:
+            for part in (0, 1):
+                first_jobs[w, target, part].wait_recv()
+                if X_FIRST[w]:
+                    add(firsts[w].at[target, part], mine[w].at[target, part])
+                else:
+                    add(firsts[w].at[target, part], (mine, theirs)[part][w].at[target, here.x])
+            if X_FIRST[w]:
+                origin, device = firsts[w].at[target, far], here.across
+            else:
+                origin, device = firsts[w].at[target, 1], here.other
+            landed = seconds[w].at[target]
+            second_jobs[w, target] = start(
+                remote(origin, landed, sends.at[w], arrivals.at[w], 8 + target, device)
+            )
+    sent.wait()
+    vec_out[...] = vec_out[...] + vec_in[1]
+    ring = [vec_send(1 + ahead, here.ring(ahead)) for ahead in (1, 2, 3)]
+
+    def lane(w, target, up):
+        at = target - 1 if up else target
+        return (rises if up else falls)[w].at[at], (12 if up else 15) + at
+
+    def receive(w, target, up):
+        slot, index = lane(w, target, up)
+        device = here.down if up else here.up
+        return remote(slot, slot, sends.at[w], arrivals.at[w], index, device)
+
+    def pass_on(w, target, up):
+        slot, index = lane(w, target, up)
+        device = here.up if up else here.down
+        return remote(seconds[w].at[target], slot, sends.at[w], arrivals.at[w], index, device)
+
+    def take_in(w, target, up):
+        receive(w, target, up).wait_recv()
+        add(seconds[w].at[target], lane(w, target, up)[0])
+
+    for target in targets:
+        for w in order:
+            second_jobs[w, target].wait_recv()
+            kept = firsts[w].at[target, here.x] if X_FIRST[w] else firsts[w].at[target, 0]
+            add(seconds[w].at[target], kept)
+            for up in (True, False):
+                if target == (0 if up else CHAIN - 1):
+                    continue
+                before = here.z < target if up else here.z > target
+                inner = here.has_down if up else here.has_up
+                pl.when(jnp.logical_and(before, inner))(
+                    lambda w=w, target=target, up=up: take_in(w, target, up)
+                )
+                start(pass_on(w, target, up), before)
+
+    for copy in ring:
+        copy.wait()
+    slots = [vec_out[...], vec_in[2], vec_in[3], vec_in[4]]
+    total = jnp.zeros_like(slots[0])
+    for at in range(CHAIN):
+        for behind in range(CHAIN):
+            same = lax.rem(here.z + CHAIN - behind, CHAIN) == at
+            total = total + jnp.where(same, slots[behind], 0.0)
+    vec_out[...] = total
+    sent = vec_send(5, here.mate)
+
+    def finish(w, target, up):
+        receive(w, target, up).wait_recv()
+        sums[w][...] += lane(w, target, up)[0][...].astype(F32)
+
+    for w in order:
+        sums[w][...] = seconds[w][here.z].astype(F32)
+        for up in (True, False):
+            for target in range(CHAIN):
+                if target != (0 if up else CHAIN - 1):
+                    pl.when(here.z == target)(
+                        lambda w=w, target=target, up=up: finish(w, target, up)
+                    )
+
+    sent.wait()
+    vec_out[0:6] = vec_out[0:6] + vec_in[5, 0:6]
+    for copy in edges:
+        pl.when(here.mp == 1)(copy.wait_recv)
+    for condition, copy in started:
+        if condition is None:
+            copy.wait_send()
+        else:
+            pl.when(condition)(copy.wait_send)
+
+
+def scatter_all(mine, theirs, vectors, out_edge, grad_edge):
+    rows = mine[0].shape[0] // (2 * CHAIN)
+    mine = [m.reshape(CHAIN, 2, rows, -1) for m in mine]
+    theirs = [t.reshape(CHAIN, 2, rows, -1) for t in theirs]
+    widths = [m.shape[-1] for m in mine]
+    vmem = pl.BlockSpec(memory_space=pltpu.VMEM)
+    shapes = [jax.ShapeDtypeStruct((rows, n), F32) for n in widths]
+    shapes += [jax.ShapeDtypeStruct(v.shape, v.dtype) for v in (vectors, out_edge, grad_edge)]
+    scratch = [pltpu.VMEM((CHAIN, 2, rows, n), BF16) for n in widths]
+    scratch += [pltpu.VMEM((CHAIN, rows, n), BF16) for n in widths]
+    scratch += [pltpu.VMEM((CHAIN - 1, rows, n), BF16) for n in widths] * 2
+    scratch += [
+        pltpu.VMEM((6,) + vectors.shape, F32),
+        pltpu.SemaphoreType.DMA((4, 18)),
+        pltpu.SemaphoreType.DMA((4, 18)),
+        pltpu.SemaphoreType.DMA((8,)),
+        pltpu.SemaphoreType.DMA((8,)),
+    ]
+    return pl.pallas_call(
+        scatter_kernel,
+        out_shape=shapes,
+        in_specs=[vmem] * 11,
+        out_specs=[vmem] * 7,
+        scratch_shapes=scratch,
+        compiler_params=pltpu.CompilerParams(
+            collective_id=1, has_side_effects=True, vmem_limit_bytes=48 * 2**20
+        ),
+        name="scatter_all",
+    )(*mine, *theirs, vectors, out_edge, grad_edge)
 
 
 def norm_stats(values):
@@ -266,12 +674,36 @@
     stages = len(grid.dims)
 
     qkv_shard = jnp.transpose(qkv_weight, (1, 0, 2)).reshape(-1, 3 * head_width).astype(BF16)
-    qkv_pair = gather_half(grid, qkv_shard, stages)
-    out_pair = gather_half(grid, out_weight.astype(BF16).T, stages - 1)
-    up_pair = gather_half(grid, up_weight.astype(BF16), stages)
-    down_pair = gather_half(grid, down_weight.astype(BF16).T, stages - 1)
-    bias_pair = (head_bias, half_swap(head_bias))
-    up_bias_pair = (up_bias, half_swap(up_bias))
+    shards = (
+        qkv_shard,
+        out_weight.astype(BF16).T,
+        up_weight.astype(BF16),
+        down_weight.astype(BF16).T,
+    )
+    units = up_weight.shape[1]
+    kernels = grid.size == 2 * CHAIN and units == width
+    if kernels:
+        flat = jnp.pad(head_bias.reshape(-1), (0, width - 2 * head_width))
+        vectors = jnp.zeros((8, width), F32).at[0].set(up_bias).at[1].set(flat)
+        *fulls, rows_both, own_cotangent, far_vectors = gather_all(
+            shards, tokens, cotangent, vectors
+        )
+        pairs = [[full[at].reshape(width, -1) for at in (0, 1)] for full in fulls]
+        qkv_pair, out_pair, up_pair, down_pair = pairs
+        far_bias = far_vectors[1, : 2 * head_width].reshape(2, head_width)
+        bias_pair, up_bias_pair = (head_bias, far_bias), (up_bias, far_vectors[0])
+        tokens_all = rows_both.reshape(2 * rows_local, width)
+        own_tokens = rows_both[0]
+    else:
+        qkv_pair = gather_half(grid, shards[0], stages)
+        out_pair = gather_half(grid, shards[1], stages - 1)
+        up_pair = gather_half(grid, shards[2], stages)
+        down_pair = gather_half(grid, shards[3], stages - 1)
+        bias_pair = (head_bias, half_swap(head_bias))
+        up_bias_pair = (up_bias, half_swap(up_bias))
+        own_tokens = bring(tokens, member)
+        own_cotangent = bring(cotangent, member)
+        tokens_all = jnp.concatenate([own_tokens, core_swap(own_tokens)], 0)
 
     slot_own, valid_own = row_table(rows_local, member, lengths)
     slot_mate, valid_mate = row_table(rows_local, mate, lengths)
@@ -285,10 +717,6 @@
 
     def settle(partial):
         return partial[:rows_local] + core_swap(partial[rows_local:].astype(BF16)).astype(F32)
-
-    own_tokens = bring(tokens, member)
-    own_cotangent = bring(cotangent, member)
-    tokens_all = share(own_tokens)
 
     heads = 2 * head_width // HEAD_DIM
     parts = []
@@ -306,34 +734,33 @@
     first = unit_one * norm_vectors[2] + norm_vectors[3]
     first_all = share(first.astype(BF16))
 
-    up_both = jnp.concatenate(up_pair, 1)
-    down_both = jnp.concatenate(down_pair, 1)
-    pre = dot(first_all, up_both, ((1,), (0,))) + jnp.concatenate(up_bias_pair)
-    phi = 0.5 * (1.0 + lax.erf(pre * (0.5**0.5)))
-    density = jnp.exp(-0.5 * pre * pre) * (1.0 / math.sqrt(2.0 * math.pi))
-    hidden = (pre * phi).astype(BF16)
-    slope = (phi + pre * density).astype(BF16)
-    ffn = settle(dot(hidden, down_both, ((1,), (1,))))
+    hiddens, slopes = [], []
+    for weight, bias in zip(up_pair, up_bias_pair):
+        pre = dot(first_all, weight, ((1,), (0,))) + bias
+        phi = 0.5 * (1.0 + lax.erf(pre * (0.5**0.5)))
+        density = jnp.exp(-0.5 * pre * pre) * (1.0 / math.sqrt(2.0 * math.pi))
+        hiddens.append((pre * phi).astype(BF16))
+        slopes.append((phi + pre * density).astype(BF16))
+    ffn = settle(
+        dot(hiddens[0], down_pair[0], ((1,), (1,))) + dot(hiddens[1], down_pair[1], ((1,), (1,)))
+    )
     unit_two, inverse_two = norm_stats(ffn + norm_vectors[1] + first)
     second = unit_two * norm_vectors[4] + norm_vectors[5]
-    layer_out = send_back(jnp.where(live, second, 0.0).astype(BF16), member)
+    layer_out = jnp.where(live, second, 0.0).astype(BF16)
 
     grad_two = jnp.where(live, own_cotangent.astype(F32), 0.0)
     d_second = norm_back(grad_two, unit_two, inverse_two, norm_vectors[4])
     d_ffn_all = share(d_second.astype(BF16))
-    d_hidden = dot(d_ffn_all, down_both, ((1,), (0,)))
-    d_pre = (d_hidden * slope.astype(F32)).astype(BF16)
-    d_first = settle(dot(d_pre, up_both, ((1,), (1,)))) + d_second
-    units = up_weight.shape[1]
-    grad_down = [
-        dot(d_ffn_all, hidden[:, at : at + units], ((0,), (0,))).astype(BF16) for at in (0, units)
+    d_pres = [
+        (dot(d_ffn_all, weight, ((1,), (0,))) * slope.astype(F32)).astype(BF16)
+        for weight, slope in zip(down_pair, slopes)
     ]
-    sum_down = scatter_sum(grid, *grad_down, True).T
-    grad_up = [
-        dot(first_all, d_pre[:, at : at + units], ((0,), (0,))).astype(BF16) for at in (0, units)
-    ]
-    sum_up = scatter_sum(grid, *grad_up, False)
-    grad_up_bias = jnp.sum(d_pre, axis=0, dtype=F32)
+    d_first = d_second + settle(
+        dot(d_pres[0], up_pair[0], ((1,), (1,))) + dot(d_pres[1], up_pair[1], ((1,), (1,)))
+    )
+    grad_down = [dot(d_ffn_all, hidden, ((0,), (0,))).astype(BF16) for hidden in hiddens]
+    grad_up = [dot(first_all, d_pre, ((0,), (0,))).astype(BF16) for d_pre in d_pres]
+    grad_up_bias = [jnp.sum(d_pre, axis=0, dtype=F32) for d_pre in d_pres]
 
     d_branch = norm_back(d_first, unit_one, inverse_one, norm_vectors[2])
     d_branch_all = share(d_branch.astype(BF16))
@@ -342,7 +769,6 @@
         dot(d_branch_all, attn[:, at : at + head_width], ((0,), (0,))).astype(BF16)
         for at in (0, head_width)
     ]
-    sum_out = scatter_sum(grid, *grad_out, True).T
     d_query, d_keys, d_values = attend_back(
         query, keys, values, allowed, log_sum, d_attn.reshape(2 * rows_local, heads, HEAD_DIM)
     )
@@ -359,13 +785,11 @@
             )
         )
     grad_qkv = [dot(tokens_all, part, ((0,), (0,))).astype(BF16) for part in d_parts]
-    sum_qkv = scatter_sum(grid, *grad_qkv, True)
-    sum_qkv = jnp.transpose(sum_qkv.reshape(-1, 3, head_width), (1, 0, 2))
     grad_bias = [jnp.sum(part, axis=0, dtype=F32) for part in d_parts]
     d_tokens = settle(
         dot(d_parts[0], qkv_pair[0], ((1,), (1,))) + dot(d_parts[1], qkv_pair[1], ((1,), (1,)))
     )
-    tokens_grad = send_back(d_tokens + d_branch, member)
+    tokens_grad = d_tokens + d_branch
 
     norm_part = jnp.stack(
         [
@@ -377,19 +801,49 @@
             jnp.sum(grad_two, axis=0),
         ]
     )
-    sum_norm = sum_all(grid, norm_part, True)
-
-    def sum_half(pair):
-        value = pair[0] + half_swap(pair[1])
-        for stage in range(stages):
-            total = value
-            for ahead in range(1, grid.dims[stage]):
-                total = total + grid.send(value, stage, ahead)
-            value = total
-        return value
-
-    sum_up_bias = sum_half((grad_up_bias[:units], grad_up_bias[units:]))
-    sum_bias = sum_half(grad_bias)
+    if kernels:
+        pad = jnp.zeros((width - 3 * head_width,), F32)
+        vectors = jnp.concatenate(
+            [
+                norm_part,
+                jnp.stack(
+                    [
+                        grad_up_bias[0],
+                        jnp.concatenate([grad_bias[0], pad]),
+                        grad_up_bias[1],
+                        jnp.concatenate([grad_bias[1], pad]),
+                    ]
+                ),
+                jnp.zeros((6, width), F32),
+            ]
+        )
+        source, free, count = move_plan(rows_local)
+        near = (grad_qkv[0], grad_out[0], grad_up[0], grad_down[0])
+        distant = (grad_qkv[1], grad_out[1], grad_up[1], grad_down[1])
+        *sums, vectors, out_back, grad_back = scatter_all(
+            near,
+            distant,
+            vectors,
+            layer_out[free : free + count],
+            tokens_grad[free : free + count],
+        )
+        sum_qkv, sum_out, sum_up, sum_down = sums
+        layer_out = put_back(layer_out, out_back, member)
+        tokens_grad = put_back(tokens_grad, grad_back, member)
+        sum_norm, sum_up_bias, sum_bias = vectors[:6], vectors[6], vectors[7]
+        sum_bias = sum_bias[: 3 * head_width]
+    else:
+        sum_qkv = scatter_sum(grid, *grad_qkv, True)
+        sum_out = scatter_sum(grid, *grad_out, True)
+        sum_up = scatter_sum(grid, *grad_up, False)
+        sum_down = scatter_sum(grid, *grad_down, True)
+        layer_out = send_back(layer_out, member)
+        tokens_grad = send_back(tokens_grad, member)
+        sum_norm = sum_all(grid, norm_part, True)
+        sum_up_bias = sum_half(grid, grad_up_bias)
+        sum_bias = sum_half(grid, grad_bias)
+    sum_qkv = jnp.transpose(sum_qkv.reshape(-1, 3, head_width), (1, 0, 2))
+    sum_out, sum_down = sum_out.T, sum_down.T
     sum_head_bias = jnp.stack([sum_bias[:head_width], sum_bias[2 * head_width :]])
 
     divisor = math.sqrt(1000.0 * grid.size * UTT)

time: 464 us -> 363 us (0.78)
  the two profiles are of different devices: /device:TPU:0 before, /device:TPU:10 now
where the time goes in v2:
time: 363 us; the launch traced here: 357 us
  Pallas kernels  171 us (47%)
  matrix products  93.4 us (26%)
  local copies, waits for them, and re-layouts  45.9 us (13%)
  other arithmetic  39.5 us (11%)
  waiting for transfers between devices  3.96 us (1%)
    pallas_call x1, Pallas kernels, scatter_all(): pl.pallas_call(scatter_kernel, out_shape=shapes, in_specs=[vmem] * 11, ou...  99.6 us
    pallas_call x1, Pallas kernels, gather_all(): pl.pallas_call(lambda *refs: gather_kernel(plan, *refs), out_shape=shapes...  71 us
    dot_general x22, matrix products, dot(): return lax.dot_general(a, b, (dims, ((), ())), preferred_element_type=F32)  50.3 us
    unnamed x196, local copies, waits for them, and re-layouts  31.1 us
    convert_element_type x1, other arithmetic, attend_back(): low = (probs * (d_probs - mean)).astype(BF16)  12.3 us
    dot_general x1, matrix products, attend_back(): jnp.einsum('qhd,khd->hqk', grad, values, preferred_element_type=F32)  11.5 us
    dot_general x1, matrix products, attend(): out = jnp.einsum('hqk,khd->qhd', low, values, preferred_element_type=F32)  9.62 us
    dot_general x1, matrix products, attend_back(): jnp.einsum('hqk,qhd->khd', probs.astype(BF16), grad, preferred_element_ty...  9.19 us
  transfers between devices with their start and end apart: 7, of which 2 were waited for; matrix products, arithmetic and copies ran while one was open for 8% of the time, Pallas kernels for 0%

profile of v2, /device:TPU:10, one launch (start us, length us, event | category | flops | bytes accessed | tf_op | source)
XLA Modules:
  0.0 357.4 jit_solution(13020475938572749685)
XLA Ops:
  9.0 71.0 %gather_all.1 = (bf16[2,8,96,576]{3,2,1,0:T(8,128)(2,1)S(1)}, bf16[2,8,96,192]{3,2,1,0:T(8,128)(2,1)S(1)}, bf16[2,8,96,768]{3,2,1,0:T(8,128)(2,1)S(1)}, bf16[2,8...) custom-call(bf16[96,576]{1,0:T(8,128)(2,1)S(1)} %copy.76.refs_0_, ...), custom_call_target="tpu_custom_call" | custom-call | tf_op jit(solution)/shard_map/gather_all/pallas_call | solution.py:403
  87.6 8.4 %fusion.93 = (f32[6,832]{1,0:T(8,128)S(1)}, f32[6,832,832]{1,2,0:T(8,128)}) fusion(bf16[832,3,3,64]{0,3,2,1:T(8,128)(2,1)S(1)} %bitcast.127, bf16[832,3,3,64]{0,3,2,1:T(8,128)(2,1)S(1)} %bitcast.122, pred[832,832]{0,1:T(8,128)(4,1)S(1)} %compare_and_fusion), kind=kOutput, calls=%fused_computation.209 | convolution fusion | flops 544722048 | bytes 21507584 | tf_op jit(solution)/shard_map/qhd,khd->hqk/dot_general | solution.py:613
  96.0 8.5 %fusion = f32[6,832]{1,0:T(8,128)S(1)} fusion(f32[6,832,832]{1,2,0:T(8,128)} %get-tuple-element.219, f32[6,832]{1,0:T(8,128)S(1)} %get-tuple-element.218), kind=kLoop, calls=%fused_computation.6 | loop fusion | flops 8301696 | bytes 16653312 | tf_op jit(solution)/shard_map/reduce_sum | solution.py:617
  104.5 9.6 %fusion.21 = bf16[6,64,832]{2,1,0:T(8,128)(2,1)S(1)} fusion(f32[6,832,832]{1,2,0:T(8,128)} %get-tuple-element.219, f32[6,832]{1,0:T(8,128)S(1)} %fusion, f32[6,832]{1,0:T(8,128)S(1)} %get-tuple-element.218, bf16[832,3,3,64]{0,3,2,1:T(8,128)(2,1)} %bitcast.123, bf16[832,3,3,64]{0,3,2,1:T(8,128)(2,1)} %bitcast.128), kind=kOutput, calls=%fused_computation.54 | convolution fusion | flops 544727040 | bytes 19209216 | tf_op jit(solution)/shard_map/hqk,khd->qhd/dot_general | solution.py:619
  115.4 2.0 collective-permute-done
  120.8 3.1 multiply_convert_fusion.4
  125.1 3.5 multiply_convert_fusion.3
  142.0 4.2 %convert_reduce_fusion.1 = (f32[768]{0:T(1024)S(1)}, bf16[832,768]{1,0:T(8,128)(2,1)S(1)}) fusion(f32[832,768]{1,0:T(8,128)} %get-tuple-element.221, f32[768]{0:T(1024)S(1)} %copy-done.76, bf16[768,768]{1,0:T(8,128)(2,1)S(1)} %bitcast.167, bf16[416,768]{1,0:T(8,128)(2,1)} %collective-permute-done.3, bf16[416,768]{1,0:T(8,128)(2,1)} %convert_element_type.201), kind=kOutput, calls=%fused_computation.25 | convolution fusion | flops 993606912 | bytes 6297600 | tf_op jit(solution)/shard_map/dot_general | solution.py:25
  146.2 3.1 convert_reduce_fusion
  153.1 3.8 %convolution_convert_fusion.2 = bf16[768,768]{1,0:T(8,128)(2,1)} fusion(bf16[832,768]{1,0:T(8,128)(2,1)S(1)} %copy-done.87, bf16[416,768]{1,0:T(8,128)(2,1)} %collective-permute-done.3, bf16[416,768]{1,0:T(8,128)(2,1)} %convert_element_type.201), kind=kOutput, calls=%fused_computation.45 | convolution fusion | flops 984612864 | bytes 3735552 | tf_op jit(solution)/shard_map/dot_general | solution.py:25
  156.9 3.8 %convolution_convert_fusion = bf16[768,768]{1,0:T(8,128)(2,1)} fusion(bf16[832,768]{1,0:T(8,128)(2,1)S(1)} %copy-done.40, bf16[416,768]{1,0:T(8,128)(2,1)} %collective-permute-done.3, bf16[416,768]{1,0:T(8,128)(2,1)} %convert_element_type.201), kind=kOutput, calls=%fused_computation.43 | convolution fusion | flops 984612864 | bytes 3735552 | tf_op jit(solution)/shard_map/dot_general | solution.py:25
  164.0 2.5 convolution_convert_fusion.1
  166.4 2.6 convolution_convert_fusion.3
  171.1 9.2 %fusion.31 = bf16[832,6,64]{0,2,1:T(8,128)(2,1)S(1)} fusion(bf16[832,6,64]{0,2,1:T(8,128)(2,1)S(1)} %bitcast.132, f32[6,832,832]{1,2,0:T(8,128)} %get-tuple-element.219, f32[6,832]{1,0:T(8,128)S(1)} %log_add_fusion), kind=kOutput, calls=%fused_computation.87 | convolution fusion | flops 540254208 | bytes 17911296 | tf_op jit(solution)/shard_map/hqk,qhd->khd/dot_general | solution.py:628
  180.4 11.5 %multiply_reduce_fusion = (f32[6,832]{1,0:T(8,128)S(1)}, f32[6,832,832]{1,2,0:T(8,128)}) fusion(f32[6,832,832]{1,2,0:T(8,128)} %get-tuple-element.219, f32[6,832]{1,0:T(8,128)S(1)} %log_add_fusion, bf16[832,6,64]{0,2,1:T(8,128)(2,1)S(1)} %bitcast.133, bf16[832,3,3,64]{0,3,2,1:T(8,128)(2,1)S(1)} %bitcast.124, bf16[832,3,3,64]{0,3,2,1:T(8,128)(2,1)S(1)} %bitcast.129), kind=kOutput, calls=%fused_computation.1 | convolution fusion | flops 544402560 | bytes 35822592 | tf_op jit(solution)/shard_map/qhd,khd->hqk/dot_general | solution.py:629
  191.9 12.3 %multiply_convert_fusion = bf16[6,832,832]{1,2,0:T(8,128)(2,1)S(1)} fusion(f32[6,832,832]{1,2,0:T(8,128)} %get-tuple-element.225, f32[6,832,832]{1,2,0:T(8,128)} %get-tuple-element.219, f32[6,832]{1,0:T(8,128)S(1)} %get-tuple-element.224, f32[6,832]{1,0:T(8,128)S(1)} %log_add_fusion), kind=kLoop, calls=%fused_computation | loop fusion | flops 16613376 | bytes 41573376 | tf_op jit(solution)/shard_map/convert_element_type | solution.py:631
  204.2 2.8 fusion.34
  210.2 2.7 fusion.67
  215.3 2.7 convolution_convert_fusion.7
  219.1 3.0 convolution_add_fusion
  224.4 2.0 convolution_convert_fusion.4
  228.0 3.3 convolution_convert_fusion.5
  234.2 2.0 fusion.22
  238.0 99.6 %scatter_all.1 = (f32[96,576]{1,0:T(8,128)S(1)}, f32[96,192]{1,0:T(8,128)S(1)}, f32[96,768]{1,0:T(8,128)S(1)}, f32[96,768]{1,0:T(8,128)S(1)}, f32[16,768]{1,0:T(...) custom-call(bf16[4,2,96,576]{3,2,1,0:T(8,128)(2,1)S(1)} %bitcast.112, ...), custom_call_target="tpu_custom_call" | custom-call | tf_op jit(solution)/shard_map/scatter_all/pallas_call | solution.py:582
  (310 shorter events, 78.1 us)
Async XLA Ops:
  0.7 6.0 %copy-start.46 = (f32[96,768]{1,0:T(8,128)S(1)}, f32[96,768]{1,0:T(8,128)}, u32[]{:S(2)}) copy-start(f32[96,768]{1,0:T(8,128)} %param.33) | copy-start | bytes 884740
  0.7 6.1 %copy-start.48 = (f32[768,96]{0,1:T(8,128)S(1)}, f32[768,96]{0,1:T(8,128)}, u32[]{:S(2)}) copy-start(f32[768,96]{0,1:T(8,128)} %param.34) | copy-start | bytes 884740
  80.0 6.4 %copy-start.5 = (bf16[2,416,768]{2,1,0:T(8,128)(2,1)}, bf16[2,416,768]{2,1,0:T(8,128)(2,1)S(1)}, u32[]{:S(2)}) copy-start(bf16[2,416,768]{2,1,0:T(8,128)(2,1)S(1)} %get-tuple-element.68) | copy-start | bytes 3833860
  81.4 5.0 %copy-start.30 = (bf16[1,8,96,576]{3,2,1,0:T(8,128)(2,1)}, bf16[1,8,96,576]{3,2,1,0:T(8,128)(2,1)S(1)}, u32[]{:S(2)}) copy-start(bf16[1,8,96,576]{3,2,1,0:T(8,128)(2,1)S(1)} %get-tuple-element.191) | copy-start | bytes 2654212
  87.6 8.4 %copy-start.17 = (bf16[832,576]{0,1:T(8,128)(2,1)}, bf16[832,576]{0,1:T(8,128)(2,1)S(1)}, u32[]{:S(2)}) copy-start(bf16[832,576]{0,1:T(8,128)(2,1)S(1)} %add_convert_fusion) | copy-start | bytes 2875396
  104.5 9.6 %copy-start.33 = (bf16[1,8,96,192]{3,2,1,0:T(8,128)(2,1)S(1)}, bf16[1,8,96,192]{3,2,1,0:T(8,128)(2,1)}, u32[]{:S(2)}) copy-start(bf16[1,8,96,192]{3,2,1,0:T(8,128)(2,1)} %get-tuple-element.196) | copy-start | bytes 884740
  115.3 2.1 collective-permute-start
  117.8 14.3 %copy-start.13 = (f32[416,768]{1,0:T(8,128)}, f32[416,768]{1,0:T(8,128)S(1)}, u32[]{:S(2)}) copy-start(f32[416,768]{1,0:T(8,128)S(1)} %get-tuple-element.185) | copy-start | bytes 3833860
  118.4 6.8 %copy-start.59 = (bf16[416,768]{1,0:T(8,128)(2,1)}, bf16[416,768]{1,0:T(8,128)(2,1)S(1)}, u32[]{:S(2)}) copy-start(bf16[416,768]{1,0:T(8,128)(2,1)S(1)} %fusion.36) | copy-start | bytes 1916932
  118.4 2.1 collective-permute-start.1
  120.5 8.2 %copy-start.28 = (bf16[1,8,96,768]{3,2,1,0:T(8,128)(2,1)}, bf16[1,8,96,768]{3,2,1,0:T(8,128)(2,1)S(1)}, u32[]{:S(2)}) copy-start(bf16[1,8,96,768]{3,2,1,0:T(8,128)(2,1)S(1)} %get-tuple-element.186) | copy-start | bytes 3538948
  129.9 2.1 collective-permute-start.2
  134.5 5.2 %copy-start.65 = (f32[3,96,192]{2,1,0:T(8,128)S(1)}, f32[3,96,192]{2,1,0:T(8,128)}, u32[]{:S(2)}) copy-start(f32[3,96,192]{2,1,0:T(8,128)} %param.45) | copy-start | bytes 663556
  135.4 6.0 %collective-permute-start.3 = (bf16[416,768]{1,0:T(8,128)(2,1)}, bf16[416,768]{1,0:T(8,128)(2,1)}, u32[]{:S(2)}, u32[]{:S(2)}) collective-permute-start(bf16[416,768]{1,0:T(8,128)(2,1)} %convert_element_type.201), channel_id=1, source_target_pairs={{0,1},{1,0},{2,3},{3,2},{4,5},{5,4},{6,7},{7,6},{8,9},{9,8},{10,11... | collective-permute-start | bytes 1916936 | tf_op jit(solution)/shard_map/ppermute | solution.py:33
  151.9 8.8 %collective-permute-start.4 = (bf16[416,768]{1,0:T(8,128)(2,1)S(1)}, bf16[416,768]{1,0:T(8,128)(2,1)S(1)}, u32[]{:S(2)}, u32[]{:S(2)}) collective-permute-start(bf16[416,768]{1,0:T(8,128)(2,1)S(1)} %slice.327), channel_id=1, source_target_pairs={{0,1},{1,0},{2,3},{3,2},{4,5},{5,4},{6,7},{7,6},{8,9},{9,8},{10,11... | collective-permute-start | bytes 1916936 | tf_op jit(solution)/shard_map/ppermute | solution.py:33
  162.1 50.9 %copy-start.61 = (bf16[416,768]{1,0:T(8,128)(2,1)}, bf16[416,768]{1,0:T(8,128)(2,1)S(1)}, u32[]{:S(2)}) copy-start(bf16[416,768]{1,0:T(8,128)(2,1)S(1)} %convert_element_type.209) | copy-start | bytes 1916932
  162.1 6.9 %collective-permute-start.5 = (bf16[416,768]{1,0:T(8,128)(2,1)S(1)}, bf16[416,768]{1,0:T(8,128)(2,1)S(1)}, u32[]{:S(2)}, u32[]{:S(2)}) collective-permute-start(bf16[416,768]{1,0:T(8,128)(2,1)S(1)} %convert_element_type.209), channel_id=1, source_target_pairs={{0,1},{1,0},{2,3},{3,2},{4,5},{5,4},{6,7},{7,6},{8,9},{9,8},{10,11... | collective-permute-start | bytes 1916936 | tf_op jit(solution)/shard_map/ppermute | solution.py:33
  171.1 9.2 %copy-start.16 = (bf16[832,576]{0,1:T(8,128)(2,1)S(1)}, bf16[832,576]{0,1:T(8,128)(2,1)}, u32[]{:S(2)}) copy-start(bf16[832,576]{0,1:T(8,128)(2,1)} %copy-done.15) | copy-start | bytes 2875396
  171.1 9.2 %copy-start.18 = (bf16[832,576]{0,1:T(8,128)(2,1)S(1)}, bf16[832,576]{0,1:T(8,128)(2,1)}, u32[]{:S(2)}) copy-start(bf16[832,576]{0,1:T(8,128)(2,1)} %copy-done.17) | copy-start | bytes 2875396
  223.1 11.1 %collective-permute-start.6 = (bf16[416,768]{1,0:T(8,128)(2,1)}, bf16[416,768]{1,0:T(8,128)(2,1)}, u32[]{:S(2)}, u32[]{:S(2)}) collective-permute-start(bf16[416,768]{1,0:T(8,128)(2,1)} %slice.326), channel_id=1, source_target_pairs={{0,1},{1,0},{2,3},{3,2},{4,5},{5,4},{6,7},{7,6},{8,9},{9,8},{10,11... | collective-permute-start | bytes 1916936 | tf_op jit(solution)/shard_map/ppermute | solution.py:33
  238.0 102.1 %copy-start.56 = (f32[192,96]{0,1:T(8,128)S(1)}, f32[192,96]{0,1:T(8,128)}, u32[]{:S(2)}) copy-start(f32[192,96]{0,1:T(8,128)} %copy-done.55) | copy-start | bytes 221188
  238.0 102.1 %copy-start.62 = (f32[192,96]{0,1:T(8,128)S(1)}, f32[192,96]{0,1:T(8,128)}, u32[]{:S(2)}) copy-start(f32[192,96]{0,1:T(8,128)} %copy.89) | copy-start | bytes 221188
  238.0 102.1 %copy-start.63 = (f32[192,96]{0,1:T(8,128)S(1)}, f32[192,96]{0,1:T(8,128)}, u32[]{:S(2)}) copy-start(f32[192,96]{0,1:T(8,128)} %copy.92) | copy-start | bytes 221188
  338.3 16.3 %copy-start.77 = (f32[768]{0:T(1024)}, f32[768]{0:T(1024)S(1)}, u32[]{:S(2)}) copy-start(f32[768]{0:T(1024)S(1)} %slice_reduce_fusion) | copy-start | bytes 9220
  (72 other events, 170.0 us)
